TPU v7x, 32 devices: a whole 2x2x4 slice. The times are simulated.
32 devices in a mesh: row: 4 (over x, core), col: 8 (over z, y).
Axes of the slice: x: 2, y: 2, z: 4, core: 2. Of those that a mesh axis runs over, the one named last changes fastest.
Arguments:
- front_panels: float32 [16, 4, 256, 8, 8, 256], P(None, 'row', 'col'), as said below
- child_update_tiles: float32 [4, 8, 8, 256, 256], P('row', 'col'), may hold values from -2 to 2
- child_rows: int32 [4, 8, 8], P('row', 'col'), may hold values from 0 to 63, as said below
- child_cols: int32 [4, 8, 8], P('row', 'col'), may hold values from 0 to 7
- child_counts: int32 [4, 8], P('row', 'col'), may hold values from 4 to 8, as said below
- row_maps: int32 [4, 8, 8, 256], P('row', 'col'), may hold values from 0 to 255, each once within a row
- col_maps: int32 [4, 8, 8, 256], P('row', 'col'), may hold values from 0 to 255, each once within a row
Outputs:
- factored_front: float32 [16, 4, 256, 8, 8, 256], P(None, 'row', None, None, 'col')
Inputs may be any that keep to these rules, and one draw needn't show every extreme that they name: child_rows[r, c, k] modulo 4 names one of four owner rows; among the live slots of one device at most 2 name the same owner row, and some device sends exactly 2 to some owner; every slot's target tile column is at most its target tile row. `child_counts`: every device of col index 0 has all slots live. `front_panels`: the diagonal of the front dominates its first tile, so that tile stays positive definite after the children are added.
All inputs are finite; a program needn't handle non-finite values.
Results may differ from a plain program's by a relative error of at most 0.0003.
Values sent between devices are 32-bit elements; how exact they have to be, the bound alone decides.
No kernel may reach another device: no remote copies, remote signals or barrier semaphores. Data moves between devices by JAX's collectives and lax.ppermute only.
A program may use at most 320 MiB of HBM per device.

v0:
```python
import functools

import jax
import jax.numpy as jnp
from jax import lax
from jax.experimental import pallas as pl
from jax.experimental.pallas import tpu as pltpu
from jax.sharding import PartitionSpec as P

HIGHEST = lax.Precision.HIGHEST
LANES = 128
VMEM_LIMIT = 60 << 20


def bf16_nt(left, right):
    return lax.dot_general(
        left, right, (((1,), (1,)), ((), ())), preferred_element_type=jnp.float32
    )


def depth_blocks(a, row_size, col_size):
    return (a * row_size + row_size - 1) // col_size + 1


def shared_blocks(a, row_size, col_size):
    return (a * row_size + row_size - 1 - col_size // 2) // col_size + 1


def move_kernel(
    row_size,
    capacity,
    ids_ref,
    rows_ref,
    cols_ref,
    count_ref,
    tiles_ref,
    row_map_ref,
    col_map_ref,
    *out_refs,
):
    slots, width = tiles_ref.shape[0], tiles_ref.shape[1]
    out_refs, lead_refs = out_refs[:row_size], out_refs[row_size:]
    chunk = width // (2 * len(lead_refs))
    labels = lax.broadcasted_iota(jnp.int32, (width, width), 0)
    count = count_ref[0]

    def one(shift, place, out_ref):
        owner = lax.rem(ids_ref[0] + shift, row_size)
        def scan(k, state):
            chosen, seen = state
            hit = (lax.rem(rows_ref[k], row_size) == owner) & (k < count)
            chosen = jnp.where(hit & (seen == place), k, chosen)
            return chosen, seen + hit.astype(jnp.int32)

        chosen, seen = lax.fori_loop(0, slots, scan, (jnp.int32(0), jnp.int32(0)))
        row_hot = (labels == row_map_ref[pl.ds(chosen, 1), :]).astype(jnp.bfloat16)
        col_hot = (labels == col_map_ref[pl.ds(chosen, 1), :]).astype(jnp.bfloat16)
        left = tiles_ref[chosen]
        tile = None
        for _ in range(3):
            term = left.astype(jnp.bfloat16)
            left = left - term.astype(jnp.float32)
            moved = jnp.dot(row_hot, term, preferred_element_type=jnp.float32)
            moved = bf16_nt(moved.astype(jnp.bfloat16), col_hot)
            tile = moved if tile is None else tile + moved
        out_ref[place] = tile
        here = (seen > place) & (cols_ref[chosen] == 0)
        target = jnp.where(here, rows_ref[chosen] // row_size, -1).astype(jnp.float32)
        mark = jnp.full((1, width), target)
        for pair, lead_ref in enumerate(lead_refs):
            for side in range(2):
                first = (2 * pair + side) * chunk
                lead_ref[side, shift, pl.ds(place * chunk, chunk), :] = tile[first : first + chunk]
                lead_ref[side, shift, pl.ds(capacity * chunk + place, 1), :] = mark

    for shift, out_ref in enumerate(out_refs):
        for place in range(capacity):
            one(shift, place, out_ref)


def move_tiles(row_size, col_size, capacity, ids, rows, cols, count, tiles, row_maps, col_maps):
    slots, width = tiles.shape[0], tiles.shape[1]
    smem = pl.BlockSpec(memory_space=pltpu.SMEM)
    vmem = pl.BlockSpec(memory_space=pltpu.VMEM)
    return pl.pallas_call(
        functools.partial(move_kernel, row_size, capacity),
        out_shape=[jax.ShapeDtypeStruct((capacity, width, width), jnp.float32)] * row_size
        + [
            jax.ShapeDtypeStruct(
                (2, row_size, capacity * (width // col_size) + 8, width), jnp.float32
            )
        ]
        * (col_size // 2),
        in_specs=[smem, smem, smem, smem, vmem, vmem, vmem],
        out_specs=[vmem] * (row_size + col_size // 2),
        compiler_params=pltpu.CompilerParams(vmem_limit_bytes=VMEM_LIMIT),
        name="move_tiles",
    )(ids, rows, cols, count, tiles, row_maps, col_maps)


def locate_kernel(row_size, capacity, slots, ids_ref, meta_ref, own_ref):
    my_row = ids_ref[0]

    def clear(n, carry):
        own_ref[0, n] = -1
        own_ref[1, n] = -1
        return carry

    lax.fori_loop(0, row_size * capacity, clear, 0)

    def source(s, carry):
        line = lax.rem(my_row + row_size - s, row_size)
        count = meta_ref[line, 2 * slots]

        def slot(k, seen):
            target = meta_ref[line, k]
            hit = (lax.rem(target, row_size) == my_row) & (k < count)

            @pl.when(hit)
            def _():
                own_ref[0, s * capacity + seen] = target // row_size
                own_ref[1, s * capacity + seen] = meta_ref[line, slots + k]

            return jnp.minimum(seen + hit.astype(jnp.int32), capacity - 1)

        lax.fori_loop(0, slots, slot, jnp.int32(0))
        return carry

    lax.fori_loop(0, row_size, source, 0)


def locate(row_size, capacity, slots, ids, meta):
    smem = pl.BlockSpec(memory_space=pltpu.SMEM)
    return pl.pallas_call(
        functools.partial(locate_kernel, row_size, capacity, slots),
        out_shape=jax.ShapeDtypeStruct((2, row_size * capacity), jnp.int32),
        in_specs=[smem, smem],
        out_specs=smem,
        name="locate",
    )(ids, meta)


def first_kernel(front_ref, out_ref, buf, sem):
    row_tiles, chunk, col_size = front_ref.shape[0], front_ref.shape[2], front_ref.shape[4]
    copies = [
        pltpu.make_async_copy(
            front_ref.at[:, 0, :, 0, :, pl.ds(half * LANES, LANES)], buf.at[half], sem.at[half]
        )
        for half in range(2)
    ]
    for copy in copies:
        copy.start()
    for copy in copies:
        copy.wait()
    for half in range(2):
        flat = buf.at[half].reshape(row_tiles * chunk * col_size, LANES)
        for a in range(row_tiles):
            out_ref[a, :, half * LANES : (half + 1) * LANES] = flat[
                pl.ds(a * chunk * col_size, chunk, stride=col_size), :
            ]


def first_rows(front):
    row_tiles, chunk, col_size, width = front.shape[0], front.shape[2], front.shape[4], front.shape[5]
    return pl.pallas_call(
        first_kernel,
        out_shape=jax.ShapeDtypeStruct((row_tiles, chunk, width), jnp.float32),
        in_specs=[pl.BlockSpec(memory_space=pltpu.HBM)],
        out_specs=pl.BlockSpec(memory_space=pltpu.VMEM),
        scratch_shapes=[
            pltpu.VMEM((2, row_tiles, chunk, col_size, LANES), jnp.float32),
            pltpu.SemaphoreType.DMA((2,)),
        ],
        compiler_params=pltpu.CompilerParams(vmem_limit_bytes=VMEM_LIMIT),
        name="first_rows",
    )(front)


def lead_kernel(capacity, own_ref, *refs):
    kids_refs, out_ref = refs[:-1], refs[-1]
    chunk = own_ref.shape[1]

    def one(a, carry):
        total = own_ref[a]
        for kids_ref in kids_refs:
            for place in range(capacity):
                kid = kids_ref[pl.ds(place * chunk, chunk), :]
                target = kids_ref[pl.ds(capacity * chunk + place, 1), :]
                total += jnp.where(target == a.astype(jnp.float32), kid, 0.0)
        out_ref[a] = total
        return carry

    lax.fori_loop(0, own_ref.shape[0], one, 0)


def lead_rows(capacity, own, kids):
    vmem = pl.BlockSpec(memory_space=pltpu.VMEM)
    return pl.pallas_call(
        functools.partial(lead_kernel, capacity),
        out_shape=jax.ShapeDtypeStruct(own.shape, jnp.float32),
        in_specs=[vmem] * (1 + len(kids)),
        out_specs=vmem,
        compiler_params=pltpu.CompilerParams(vmem_limit_bytes=VMEM_LIMIT),
        name="lead_rows",
    )(own, *kids)


def order_kernel(ids_ref, *refs):
    same, other_ref, out_ref = refs[:-2], refs[-2], refs[-1]
    for k, same_ref in enumerate(same):
        out_ref[lax.bitwise_xor(ids_ref[1], 2 * k)] = same_ref[...]
        out_ref[lax.bitwise_xor(ids_ref[1], 2 * k + 1)] = other_ref[k]


def order_rows(ids, same, other):
    smem = pl.BlockSpec(memory_space=pltpu.SMEM)
    vmem = pl.BlockSpec(memory_space=pltpu.VMEM)
    return pl.pallas_call(
        order_kernel,
        out_shape=jax.ShapeDtypeStruct((2 * len(same),) + same[0].shape, jnp.float32),
        in_specs=[smem] + [vmem] * (1 + len(same)),
        out_specs=vmem,
        compiler_params=pltpu.CompilerParams(vmem_limit_bytes=VMEM_LIMIT),
        name="order_rows",
    )(ids, *same, other)


def halves_of(value):
    high = value.astype(jnp.bfloat16)
    return high, (value - high.astype(jnp.float32)).astype(jnp.bfloat16)


def panel_kernel(ids_ref, inverse_ref, factor_ref, rows_ref, cols_ref, row_out, high_out, low_out):
    width = inverse_ref.shape[0]
    high, low = halves_of(inverse_ref[...])

    def solve(tile):
        tile_high, tile_low = halves_of(tile)
        return bf16_nt(tile_high, high) + (bf16_nt(tile_high, low) + bf16_nt(tile_low, high))

    def row(a, carry):
        row_out[a] = solve(rows_ref[:, a].reshape(width, width))
        return carry

    lax.fori_loop(0, row_out.shape[0], row, 0)

    @pl.when(ids_ref[0] == 0)
    def _():
        row_out[0] = factor_ref[...]

    def column(b, carry):
        col = solve(cols_ref[:, b].reshape(width, width))
        high_out[b], low_out[b] = halves_of(col)
        return carry

    lax.fori_loop(0, high_out.shape[0], column, 0)


def panels(ids, inverse, factor, rows, cols):
    smem = pl.BlockSpec(memory_space=pltpu.SMEM)
    vmem = pl.BlockSpec(memory_space=pltpu.VMEM)
    width = inverse.shape[0]
    return pl.pallas_call(
        panel_kernel,
        out_shape=(
            jax.ShapeDtypeStruct((rows.shape[1], width, width), jnp.float32),
            jax.ShapeDtypeStruct((cols.shape[1], width, width), jnp.bfloat16),
            jax.ShapeDtypeStruct((cols.shape[1], width, width), jnp.bfloat16),
        ),
        in_specs=[smem, vmem, vmem, vmem, vmem],
        out_specs=(vmem, vmem, vmem),
        compiler_params=pltpu.CompilerParams(vmem_limit_bytes=VMEM_LIMIT),
        name="panels",
    )(ids, inverse, factor, rows, cols)


def pack_kernel(depths, counts, front_ref, out_ref, in_buf, out_buf, in_sem, out_sem):
    col_size = front_ref.shape[4]
    chunk = front_ref.shape[2]

    def fetch(i):
        a, nb, slot = depths[i], counts[i], i % 2
        return [
            pltpu.make_async_copy(
                front_ref.at[a, 0, :, pl.ds(0, nb), :, pl.ds(half * LANES, LANES)],
                in_buf.at[slot, half, :, pl.ds(0, nb)],
                in_sem.at[slot, half],
            )
            for half in range(2)
        ]

    def send(i):
        first, nb, slot = sum(counts[:i]), counts[i], i % 2
        return pltpu.make_async_copy(
            out_buf.at[slot, :, pl.ds(0, nb)], out_ref.at[:, pl.ds(first, nb)], out_sem.at[slot]
        )

    steps = len(depths)
    for copy in fetch(0):
        copy.start()
    for i in range(steps):
        slot, nb = i % 2, counts[i]
        if i + 1 < steps:
            for copy in fetch(i + 1):
                copy.start()
        for copy in fetch(i):
            copy.wait()
        if i >= 2:
            send(i - 2).wait()
        for half in range(2):
            total = in_buf.shape[3]
            flat = in_buf.at[slot, half].reshape(chunk * total * col_size, LANES)
            for b in range(nb):
                for c in range(col_size):
                    out_buf[slot, c, b, :, half * LANES : (half + 1) * LANES] = flat[
                        pl.ds(b * col_size + c, chunk, stride=total * col_size), :
                    ]
        send(i).start()
    for i in range(max(steps - 2, 0), steps):
        send(i).wait()


def pack(front, depths, counts):
    chunk, col_size, width = front.shape[2], front.shape[4], front.shape[5]
    most = max(counts)
    return pl.pallas_call(
        functools.partial(pack_kernel, depths, counts),
        out_shape=jax.ShapeDtypeStruct((col_size, sum(counts), chunk, width), jnp.float32),
        in_specs=[pl.BlockSpec(memory_space=pltpu.HBM)],
        out_specs=pl.BlockSpec(memory_space=pltpu.HBM),
        scratch_shapes=[
            pltpu.VMEM((2, 2, chunk, most, col_size, LANES), jnp.float32),
            pltpu.VMEM((2, col_size, most, chunk, width), jnp.float32),
            pltpu.SemaphoreType.DMA((2, 2)),
            pltpu.SemaphoreType.DMA((2,)),
        ],
        compiler_params=pltpu.CompilerParams(vmem_limit_bytes=VMEM_LIMIT),
        name="pack",
    )(front)


def edge_kernel(blocks, ids_ref, front_ref, *refs):
    out_refs, (buf, sem) = refs[:-2], refs[-2:]
    chunk, col_size = front_ref.shape[2], front_ref.shape[4]
    copies = [
        pltpu.make_async_copy(
            front_ref.at[a, 0, :, b, :, pl.ds(half * LANES, LANES)], buf.at[i, half], sem.at[i, half]
        )
        for i, (a, b) in enumerate(blocks)
        for half in range(2)
    ]
    for copy in copies:
        copy.start()
    for copy in copies:
        copy.wait()
    for i in range(len(blocks)):
        for half in range(2):
            flat = buf.at[i, half].reshape(chunk * col_size, LANES)
            for k, out_ref in enumerate(out_refs):
                out_ref[i, :, half * LANES : (half + 1) * LANES] = flat[
                    pl.ds(lax.bitwise_xor(ids_ref[1], k), chunk, stride=col_size), :
                ]


def pack_edge(ids, front, blocks):
    chunk, col_size, width = front.shape[2], front.shape[4], front.shape[5]
    vmem = pl.BlockSpec(memory_space=pltpu.VMEM)
    return pl.pallas_call(
        functools.partial(edge_kernel, blocks),
        out_shape=[jax.ShapeDtypeStruct((len(blocks), chunk, width), jnp.float32)] * col_size,
        in_specs=[pl.BlockSpec(memory_space=pltpu.SMEM), pl.BlockSpec(memory_space=pltpu.HBM)],
        out_specs=[vmem] * col_size,
        scratch_shapes=[
            pltpu.VMEM((len(blocks), 2, chunk, col_size, LANES), jnp.float32),
            pltpu.SemaphoreType.DMA((len(blocks), 2)),
        ],
        compiler_params=pltpu.CompilerParams(vmem_limit_bytes=VMEM_LIMIT),
        name="pack_edge",
    )(ids, front)


def finish_kernel(
    depths,
    shared,
    edges,
    row_size,
    col_size,
    ids_ref,
    own_ref,
    recv_ref,
    rows_ref,
    high_ref,
    low_ref,
    kids_ref,
    *rest,
):
    edge_refs = rest[:col_size]
    out_ref, in_buf, row_buf, out_buf, high_buf, low_buf, kid_buf, *sems = rest[-13:]
    in_sem, row_sem, out_sem, col_sem, kid_sem, edge_sem = sems
    my_row, my_col = ids_ref[0], ids_ref[1]
    width = high_ref.shape[1]
    chunk = width // col_size
    halves = width // LANES
    blocks = high_ref.shape[0]
    stride = blocks * halves

    counts = [n + (edge is not None) for n, edge in zip(shared, edges)]

    def fetch(i):
        a, nb, edge, slot, first = depths[i], shared[i], edges[i], i % 2, sum(shared[:i])
        copies = [pltpu.make_async_copy(rows_ref.at[a], row_buf.at[slot], row_sem.at[slot])]
        if nb:
            copies.append(
                pltpu.make_async_copy(
                    recv_ref.at[:, pl.ds(first, nb)],
                    in_buf.at[slot, :, pl.ds(0, nb)],
                    in_sem.at[slot],
                )
            )
        if edge is not None:
            for k, edge_ref in enumerate(edge_refs):
                copies.append(
                    pltpu.make_async_copy(
                        edge_ref.at[edge],
                        in_buf.at[slot, lax.bitwise_xor(my_col, k), nb],
                        edge_sem.at[slot, k],
                    )
                )
        return copies

    def send(i):
        return pltpu.make_async_copy(out_buf.at[i % 2], out_ref.at[depths[i]], out_sem.at[i % 2])

    most = high_buf.shape[0]
    columns = [
        pltpu.make_async_copy(high_ref.at[pl.ds(0, most)], high_buf, col_sem.at[0]),
        pltpu.make_async_copy(low_ref.at[pl.ds(0, most)], low_buf, col_sem.at[1]),
    ]
    steps = len(depths)
    for copy in (*fetch(0), *columns):
        copy.start()
    for i in range(steps):
        a, nb, slot = depths[i], counts[i], i % 2
        if i + 1 < steps:
            for copy in fetch(i + 1):
                copy.start()
        for copy in fetch(i):
            copy.wait()
        if i == 0:
            for copy in columns:
                copy.wait()
        if i >= 2:
            send(i - 2).wait()
        for n in range(kids_ref.shape[0]):

            @pl.when(own_ref[0, n] == a)
            def _():
                copy = pltpu.make_async_copy(kids_ref.at[n], kid_buf, kid_sem)
                copy.start()
                copy.wait()
                in_buf[slot, :, own_ref[1, n]] += kid_buf[...].reshape(col_size, chunk, width)

        tile_i = a * row_size + my_row

        def store(b, tile):
            for half in range(halves):
                out_buf[slot, pl.ds(b * halves + half, width, stride=stride), :] = tile[
                    :, half * LANES : (half + 1) * LANES
                ]

        row_high, row_low = halves_of(row_buf[slot])

        def update(b):
            return bf16_nt(row_high, high_buf[b]) + (
                bf16_nt(row_high, low_buf[b]) + bf16_nt(row_low, high_buf[b])
            )

        for b in range(nb):
            tile = in_buf[slot, :, b].reshape(width, width)
            tile_j = b * col_size + my_col
            if b < nb - 1:
                store(b, tile - update(b))
            else:

                @pl.when(tile_i > tile_j)
                def _():
                    store(b, tile - update(b))

                @pl.when(tile_i == tile_j)
                def _():
                    store(b, 0.5 * (tile + tile.T) - update(b))

                @pl.when(tile_i < tile_j)
                def _():
                    store(b, jnp.zeros_like(tile))

        @pl.when(my_col == 0)
        def _():
            store(0, row_buf[slot])

        zero = jnp.zeros((width, LANES), jnp.float32)
        for n in range(nb * halves, stride):
            out_buf[slot, pl.ds(n, width, stride=stride), :] = zero
        send(i).start()
    for i in range(max(steps - 2, 0), steps):
        send(i).wait()


def finish(
    depths, shared, edges, row_size, col_size, ids, own, recv, rows, high, low, kids, edge, out=None
):
    smem = pl.BlockSpec(memory_space=pltpu.SMEM)
    hbm = pl.BlockSpec(memory_space=pltpu.HBM)
    blocks, width = high.shape[0], high.shape[1]
    chunk = width // col_size
    lines = width * blocks * (width // LANES)
    counts = [n + (edge is not None) for n, edge in zip(shared, edges)]
    operands = [ids, own, recv, rows, high, low, kids, *edge]
    in_specs = [smem, smem] + [hbm] * (5 + len(edge))
    aliases = {}
    if out is not None:
        operands.append(out)
        in_specs.append(hbm)
        aliases = {len(operands) - 1: 0}
    return pl.pallas_call(
        functools.partial(finish_kernel, depths, shared, edges, row_size, col_size),
        out_shape=jax.ShapeDtypeStruct((rows.shape[0], lines, LANES), jnp.float32),
        in_specs=in_specs,
        out_specs=hbm,
        scratch_shapes=[
            pltpu.VMEM((2, col_size, max(counts), chunk, width), jnp.float32),
            pltpu.VMEM((2, width, width), jnp.float32),
            pltpu.VMEM((2, lines, LANES), jnp.float32),
            pltpu.VMEM((max(counts), width, width), jnp.bfloat16),
            pltpu.VMEM((max(counts), width, width), jnp.bfloat16),
            pltpu.VMEM((width, width), jnp.float32),
            pltpu.SemaphoreType.DMA((2,)),
            pltpu.SemaphoreType.DMA((2,)),
            pltpu.SemaphoreType.DMA((2,)),
            pltpu.SemaphoreType.DMA((2,)),
            pltpu.SemaphoreType.DMA,
            pltpu.SemaphoreType.DMA((2, col_size)),
        ],
        input_output_aliases=aliases,
        compiler_params=pltpu.CompilerParams(vmem_limit_bytes=VMEM_LIMIT),
        name="finish",
    )(*operands)


def factor_and_inverse(corner):
    size = corner.shape[0] // 2
    eye = jnp.eye(size, dtype=jnp.float32)

    def both(block):
        factor = lax.linalg.cholesky(block, symmetrize_input=False)
        return factor, jax.scipy.linalg.solve_triangular(factor, eye, lower=True)

    def product(left, right):
        return jnp.dot(left, right, precision=HIGHEST)

    top, top_inverse = both(corner[:size, :size])
    below = product(corner[size:, :size], top_inverse.T)
    end, end_inverse = both(corner[size:, size:] - product(below, below.T))
    corner_inverse = -product(end_inverse, product(below, top_inverse))
    zero = jnp.zeros_like(eye)
    return (
        jnp.block([[top, zero], [below, end]]),
        jnp.block([[top_inverse, zero], [corner_inverse, end_inverse]]),
    )


def on_device(front, child_tiles, child_rows, child_cols, child_counts, row_maps, col_maps):
    row_size, col_size = lax.axis_size("row"), lax.axis_size("col")
    my_row, my_col = lax.axis_index("row"), lax.axis_index("col")
    row_tiles, chunk, col_tiles, width = front.shape[0], front.shape[2], front.shape[3], front.shape[5]
    slots = child_tiles.shape[2]
    capacity = slots // 4
    arrivals = row_size * capacity
    group = col_size // row_size
    ids = jnp.stack([my_row, my_col]).astype(jnp.int32)

    shared = [shared_blocks(a, row_size, col_size) for a in range(row_tiles)]
    edge_blocks = [
        (a, shared[a]) for a in range(row_tiles) if depth_blocks(a, row_size, col_size) > shared[a]
    ]
    edge_of = {a: i for i, (a, _) in enumerate(edge_blocks)}
    last = (row_tiles - 5) * 3 // 4 + 1
    parts = [[row_tiles - 2], [row_tiles - 1, row_tiles - 3, row_tiles - 4]]
    parts.append([a for a in range(row_tiles - 5, -1, -1) if a != last])
    parts.append([last])

    def packed(part, *after):
        held = lax.optimization_barrier((front,) + after)[0]
        sent = [a for a in part if shared[a]]
        return pack(held, sent, [shared[a] for a in sent])

    def exchange(blocks, *after):
        blocks = lax.optimization_barrier((blocks,) + after)[0]
        return lax.all_to_all(blocks, "col", split_axis=0, concat_axis=0, tiled=True)

    def along_row(shift):
        return [(r, (r + shift) % row_size) for r in range(row_size)]

    def across_col(k):
        return [(c, c ^ k) for c in range(col_size)]

    moved = move_tiles(
        row_size,
        col_size,
        capacity,
        ids,
        child_rows.reshape(slots),
        child_cols.reshape(slots),
        child_counts.reshape(1),
        child_tiles.reshape(slots, width, width),
        row_maps.reshape(slots, width),
        col_maps.reshape(slots, width),
    )
    moved, pieces = moved[:row_size], moved[row_size:]

    sent = [
        lax.ppermute(pieces[pair], "col", [(0, 2 * pair)]) for pair in range(1, col_size // 2)
    ]
    edge = pack_edge(ids, lax.optimization_barrier((front, pieces[0]))[0], edge_blocks)

    def send_edge(k, value):
        steps = [
            (r * col_size + c, r * col_size + (c ^ k))
            for r in range(row_size)
            for c in range(col_size)
            if c ^ k <= r
        ]
        return lax.ppermute(value, ("row", "col"), steps)

    half = col_size // 2
    far = [send_edge(k, edge[k]) for k in range(half, col_size)]
    second = packed(parts[1], pieces[0])
    blocks = packed(parts[0], pieces[0])
    first = first_rows(front)
    *sent, blocks, _ = lax.optimization_barrier((*sent, blocks, *far[:1]))
    arrived = [exchange(blocks, *sent, *far)]
    lead = jnp.where(my_col == 0, pieces[0], sum(sent[1:], sent[0]))
    other = lax.ppermute(lead[1], "col", [(c, c + 1) for c in range(0, col_size, 2)])
    other, second, first = lax.optimization_barrier((other, second, first))
    lead = jnp.where(my_col % 2 == 0, lead[0], other)
    lead = [lead[0]] + [
        lax.ppermute(lead[shift], "row", along_row(shift)) for shift in range(1, row_size)
    ]
    raw = lead_rows(capacity, first, lead)

    steps = range(2, half, 2)
    across = lax.ppermute(raw, "col", across_col(half))
    inner = [lax.ppermute(raw, "col", across_col(k)) for k in steps]
    near = [send_edge(k, lax.optimization_barrier((edge[k], raw))[0]) for k in range(1, half)]
    arrived.append(exchange(second, arrived[0], across, *inner, *near))
    outer = [lax.ppermute(across, "col", across_col(k)) for k in steps]
    known = [raw, *inner, across]
    third = packed(parts[2], across)
    stacked, third = lax.optimization_barrier((jnp.stack(known), third))
    beside = lax.ppermute(stacked, "col", across_col(1))
    outside = lax.ppermute(jnp.stack(outer), "col", across_col(1))
    raw_rows = order_rows(ids, known + outer, jnp.concatenate([beside, outside]))
    meta = jnp.concatenate(
        [child_rows.reshape(1, slots), child_cols.reshape(1, slots), child_counts.reshape(1, 1)], axis=1
    )
    meta, _ = lax.optimization_barrier((meta, across))
    meta = lax.all_gather(meta, "row", axis=0, tiled=True)
    own = locate(row_size, capacity, slots, ids, meta)
    *moved, _ = lax.optimization_barrier((*moved, across))
    kids = jnp.concatenate(
        [moved[0]]
        + [lax.ppermute(moved[shift], "row", along_row(shift)) for shift in range(1, row_size)]
    )

    arrived.append(exchange(third, arrived[1], beside, outside, own, kids))
    edge = [edge[0], *near, *far]

    corner_mine = corner = raw_rows[:, 0].reshape(width, width)
    corner = jnp.where(my_row == 0, corner, 0.0)
    for shift in range(1, row_size):
        corner = corner + lax.ppermute(corner_mine, "row", [(0, shift)])
    corner = 0.5 * (corner + corner.T)
    factor, inverse = factor_and_inverse(corner)

    mine = lax.dynamic_index_in_dim(
        raw_rows.reshape(col_size, col_tiles, group, chunk, width),
        my_col // row_size,
        2,
        keepdims=False,
    )
    raw_cols = jnp.where(my_row == my_col % row_size, mine, 0.0)
    for shift in range(1, row_size):
        steps = [
            ((c % row_size) * col_size + c, ((c + shift) % row_size) * col_size + c)
            for c in range(col_size)
        ]
        raw_cols = raw_cols + lax.ppermute(mine, ("row", "col"), steps)
    rows, high, low = panels(ids, inverse, factor, raw_rows, raw_cols)

    out = None
    for step, part in enumerate(parts):
        if step == 2:
            arrived.append(exchange(packed(parts[3]), arrived[2], out))
        out = finish(
            part,
            [shared[a] for a in part],
            [edge_of.get(a) for a in part],
            row_size,
            col_size,
            ids,
            own,
            arrived[step],
            rows,
            high,
            low,
            kids,
            edge,
            out,
        )
    return out.reshape(row_tiles, 1, width, col_tiles, 1, width)


def solution(mesh):
    return jax.shard_map(
        on_device,
        mesh=mesh,
        in_specs=(
            P(None, "row", "col", None, None, None),
            P("row", "col", None, None, None),
            P("row", "col", None),
            P("row", "col", None),
            P("row", "col"),
            P("row", "col", None, None),
            P("row", "col", None, None),
        ),
        out_specs=P(None, "row", None, None, "col", None),
        check_vma=False,
    )
```

profile of v0, /device:TPU:6, one launch (start us, length us, event | category | flops | bytes accessed | tf_op | source)
XLA Modules:
  0.0 488.8 jit_solution(1019749921743021500)
XLA Ops:
  1.3 8.4 %move_tiles.1 = (f32[2,256,256]{2,1,0:T(8,128)}, f32[2,256,256]{2,1,0:T(8,128)}, f32[2,256,256]{2,1,0:T(8,128)}, f32[2,256,256]{2,1,0:T(8,128)}, f32[2,4,72,256]...) custom-call(s32[2]{0:T(128)} %pad_add_fusion.ids_ref, ...), custom_call_target="tpu_custom_call" | custom-call | tf_op jit(solution)/shard_map/move_tiles/pallas_call | solution.py:85
  18.7 18.0 %collective-permute-done.3.rest_4_ = f32[8,32,256]{2,1,0:T(8,128)S(1)} collective-permute-done((f32[8,32,256]{2,1,0:T(8,128)}, f32[8,32,256]{2,1,0:T(8,128)S(1)}, u32[]{:S(2)}, u32[]{:S(2)}) %collective-permute-start.3) | collective-permute-done | bytes 262176 | tf_op jit(solution)/shard_map/ppermute | solution.py:633
  42.8 6.2 %collective-permute-done.11.rest_6_ = f32[8,32,256]{2,1,0:T(8,128)S(1)} collective-permute-done((f32[8,32,256]{2,1,0:T(8,128)}, f32[8,32,256]{2,1,0:T(8,128)S(1)}, u32[]{:S(2)}, u32[]{:S(2)}) %collective-permute-start.11) | collective-permute-done | bytes 262176 | tf_op jit(solution)/shard_map/ppermute | solution.py:633
  49.0 6.1 %collective-permute-done.12.rest_7_ = f32[8,32,256]{2,1,0:T(8,128)} collective-permute-done((f32[8,32,256]{2,1,0:T(8,128)}, f32[8,32,256]{2,1,0:T(8,128)}, u32[]{:S(2)}, u32[]{:S(2)}) %collective-permute-start.12) | collective-permute-done | bytes 262176 | tf_op jit(solution)/shard_map/ppermute | solution.py:633
  55.1 7.5 %all-to-all-start = ((f32[8,7,32,256]{3,2,1,0:T(8,128)}), f32[8,7,32,256]{3,2,1,0:T(8,128)S(1)}, u32[]{:S(2)}, u32[]{:S(2)}) async-start(f32[8,7,32,256]{3,2,1,0:T(8,128)} %pack.4), calls=%async_computation | async-start | bytes 3670016 | tf_op jit(solution)/shard_map/all_to_all | solution.py:599
  69.4 7.5 %pack.5 = f32[8,21,32,256]{3,2,1,0:T(8,128)} custom-call(f32[16,1,32,8,8,256]{5,4,3,2,1,0:T(8,128)} %front_ref.6), custom_call_target="tpu_custom_call" | custom-call | tf_op jit(solution)/shard_map/pack/pallas_call | solution.py:326
  76.9 8.1 %collective-permute-done.4 = f32[4,72,256]{2,1,0:T(8,128)S(1)} collective-permute-done((f32[4,72,256]{2,1,0:T(8,128)}, f32[4,72,256]{2,1,0:T(8,128)S(1)}, u32[]{:S(2)}, u32[]{:S(2)}) %collective-permute-start.4) | collective-permute-done | bytes 294944 | tf_op jit(solution)/shard_map/ppermute | solution.py:643
  105.5 6.0 %collective-permute-start.15 = (f32[8,32,256]{2,1,0:T(8,128)}, f32[8,32,256]{2,1,0:T(8,128)S(1)}, u32[]{:S(2)}, u32[]{:S(2)}) collective-permute-start(f32[8,32,256]{2,1,0:T(8,128)} %get-tuple-element.74), channel_id=1, source_target_pairs={{3,0},{10,9},{11,8},{17,18},{18,17},{19,16},{24,27},{25,26},{26,25... | collective-permute-start | bytes 786440 | tf_op jit(solution)/shard_map/ppermute | solution.py:633
  111.6 21.7 %collective-permute-done.14.rest_2_ = f32[8,32,256]{2,1,0:T(8,128)S(1)} collective-permute-done((f32[8,32,256]{2,1,0:T(8,128)}, f32[8,32,256]{2,1,0:T(8,128)S(1)}, u32[]{:S(2)}, u32[]{:S(2)}) %collective-permute-start.14) | collective-permute-done | bytes 262176 | tf_op jit(solution)/shard_map/ppermute | solution.py:633
  133.2 5.9 %collective-permute-done.15.rest_3_ = f32[8,32,256]{2,1,0:T(8,128)S(1)} collective-permute-done((f32[8,32,256]{2,1,0:T(8,128)}, f32[8,32,256]{2,1,0:T(8,128)S(1)}, u32[]{:S(2)}, u32[]{:S(2)}) %collective-permute-start.15) | collective-permute-done | bytes 262176 | tf_op jit(solution)/shard_map/ppermute | solution.py:633
  145.5 10.3 %pack.7 = f32[8,31,32,256]{3,2,1,0:T(8,128)} custom-call(f32[16,1,32,8,8,256]{5,4,3,2,1,0:T(8,128)} %front_ref.6), custom_call_target="tpu_custom_call" | custom-call | tf_op jit(solution)/shard_map/pack/pallas_call | solution.py:326
  161.0 84.1 %collective-permute-done.17.refs_3_ = f32[16,32,256]{2,1,0:T(8,128)S(1)} collective-permute-done((f32[16,32,256]{2,1,0:T(8,128)}, f32[16,32,256]{2,1,0:T(8,128)S(1)}, u32[]{:S(2)}, u32[]{:S(2)}) %collective-permute-start.17) | collective-permute-done | bytes 524320 | tf_op jit(solution)/shard_map/ppermute | solution.py:656
  290.9 11.7 %custom-call.8 = f32[128,128]{1,0:T(8,128)S(1)} custom-call(f32[128,128]{1,0:T(8,128)S(1)} %slice.53), custom_call_target="Cholesky" | custom-call | tf_op jit(solution)/shard_map/cholesky/custom-call.1 | solution.py:555
  304.0 9.8 %custom-call.9 = f32[1,128,128]{1,2,0:T(8,128)S(1)} custom-call(f32[1,128,128]{2,1,0:T(8,128)S(1)} %get-tuple-element.93), custom_call_target="InvertDiagBlocksLowerTriangular" | custom-call | tf_op jit(solution)/shard_map/jit(_solve_triangular)/triangular_solve | solution.py:556
  314.8 11.7 %custom-call.10 = f32[128,128]{1,0:T(8,128)S(1)} custom-call(f32[128,128]{1,0:T(8,128)S(1)} %slice_subtract_fusion), custom_call_target="Cholesky" | custom-call | tf_op jit(solution)/shard_map/cholesky/custom-call.1 | solution.py:555
  327.9 18.5 %custom-call.11 = f32[1,128,128]{1,2,0:T(8,128)S(1)} custom-call(f32[1,128,128]{2,1,0:T(8,128)S(1)} %get-tuple-element.91), custom_call_target="InvertDiagBlocksLowerTriangular" | custom-call | tf_op jit(solution)/shard_map/jit(_solve_triangular)/triangular_solve | solution.py:556
  348.2 6.0 %add_add_fusion.cols_ref = f32[8,8,32,256]{3,2,1,0:T(8,128)} fusion(f32[8,8,32,256]{3,2,1,0:T(8,128)} %collective-permute-done.27, f32[8,8,32,256]{3,2,1,0:T(8,128)} %collective-permute-done.26, f32[8,8,32,256]{3,2,1,0:T(8,128)} %collective-permute-done.25, pred[]{:T(512)S(6)} %eq.24, f32[8,8,2,32,256]{4,3,2,1,0:T(8,128)} %bitcast.62, s32[]{:T(128)S(6)} %select_n.69), kind=kLoop, calls=%fused_computation.1 | loop fusion | flops 2097152 | bytes 10485765 | tf_op jit(solution)/shard_map/add | solution.py:697
  354.2 12.9 %panels.1 = (f32[16,256,256]{2,1,0:T(8,128)}, bf16[8,256,256]{2,1,0:T(8,128)(2,1)}, bf16[8,256,256]{2,1,0:T(8,128)(2,1)}) custom-call(s32[2]{0:T(128)} %pad_add_fusion.ids_ref, f32[256,256]{1,0:T(8,128)} %get-tuple-element.100.inverse_ref, f32[256,256]{1,0:T(8,128)} %get-tuple-element.99.factor_ref, f32[8,16,32,256]{3,2,1,0:T(8,128)} %order_rows.1.rows_ref, ...), custom_call_target="tpu_custom_call" | custom-call | tf_op jit(solution)/shard_map/panels/pallas_call | solution.py:263
  367.1 8.1 %finish.4.rest_8_ = f32[16,4096,128]{2,1,0:T(8,128)} custom-call(s32[2]{0:T(128)} %pad_add_fusion.ids_ref, s32[2,8]{1,0:T(2,128)} %locate.1.own_ref, f32[8,7,32,256]{3,2,1,0:T(8,128)} %copy-done.1, f32[16,256,256]{2,1,0:T(8,128)} %get-tuple-element.86.rows_ref, bf16[8,256,256]{2,1,0:T(8,128)(2,1)} %get-tuple-element.87.high_ref, ...), custom_call_target="tpu_custom_call" | custom-call | tf_op jit(solution)/shard_map/finish/pallas_call | solution.py:525
  375.2 11.3 %finish.5.rest_8_ = f32[16,4096,128]{2,1,0:T(8,128)} custom-call(s32[2]{0:T(128)} %pad_add_fusion.ids_ref, s32[2,8]{1,0:T(2,128)} %locate.1.own_ref, f32[8,21,32,256]{3,2,1,0:T(8,128)} %all-to-all-done.1.recv_ref, f32[16,256,256]{2,1,0:T(8,128)} %get-tuple-element.86.rows_ref, ...), custom_call_target="tpu_custom_call", output_to_operand_aliasing={{}: (15, {})} | custom-call | tf_op jit(solution)/shard_map/finish/pallas_call | solution.py:525
  386.5 58.8 %all-to-all-done.2.recv_ref = f32[8,31,32,256]{3,2,1,0:T(8,128)} async-done(((f32[8,31,32,256]{3,2,1,0:T(8,128)}), f32[8,31,32,256]{3,2,1,0:T(8,128)}, u32[]{:S(2)}, u32[]{:S(2)}) %all-to-all-start.2) | async-done | bytes 8126496 | tf_op jit(solution)/shard_map/all_to_all | solution.py:599
  449.7 25.5 %finish.6.rest_8_ = f32[16,4096,128]{2,1,0:T(8,128)} custom-call(s32[2]{0:T(128)} %pad_add_fusion.ids_ref, s32[2,8]{1,0:T(2,128)} %locate.1.own_ref, f32[8,31,32,256]{3,2,1,0:T(8,128)} %all-to-all-done.2.recv_ref, f32[16,256,256]{2,1,0:T(8,128)} %get-tuple-element.86.rows_ref, ...), custom_call_target="tpu_custom_call", output_to_operand_aliasing={{}: (15, {})} | custom-call | tf_op jit(solution)/shard_map/finish/pallas_call | solution.py:525
  475.1 5.5 %all-to-all-done.3.recv_ref = f32[8,5,32,256]{3,2,1,0:T(8,128)S(1)} async-done(((f32[8,5,32,256]{3,2,1,0:T(8,128)}), f32[8,5,32,256]{3,2,1,0:T(8,128)S(1)}, u32[]{:S(2)}, u32[]{:S(2)}) %all-to-all-start.3) | async-done | bytes 1310752 | tf_op jit(solution)/shard_map/all_to_all | solution.py:599
  481.7 6.6 %finish.7 = f32[16,4096,128]{2,1,0:T(8,128)} custom-call(s32[2]{0:T(128)} %pad_add_fusion.ids_ref, s32[2,8]{1,0:T(2,128)} %locate.1.own_ref, f32[8,5,32,256]{3,2,1,0:T(8,128)} %copy-done.2, f32[16,256,256]{2,1,0:T(8,128)} %get-tuple-element.86.rows_ref, bf16[8,256,256]{2,1,0:T(8,128)(2,1)} %get-tuple-element.87.high_ref, ...), custom_call_target="tpu_custom_call", output_to_operand_aliasing={{}: (15, {})} | custom-call | tf_op jit(solution)/shard_map/finish/pallas_call | solution.py:525
  (137 shorter events, 110.9 us)
Async XLA Ops:
  9.7 28.3 %collective-permute-start = (f32[2,4,72,256]{3,2,1,0:T(8,128)}, f32[2,4,72,256]{3,2,1,0:T(8,128)S(1)}, u32[]{:S(2)}, u32[]{:S(2)}) collective-permute-start(f32[2,4,72,256]{3,2,1,0:T(8,128)} %get-tuple-element.50), channel_id=1, source_target_pairs={{0,2},{8,10},{16,18},{24,26}} | collective-permute-start | bytes 1769480 | tf_op jit(solution)/shard_map/ppermute | solution.py:622
  10.4 32.1 %collective-permute-start.1 = (f32[2,4,72,256]{3,2,1,0:T(8,128)}, f32[2,4,72,256]{3,2,1,0:T(8,128)S(1)}, u32[]{:S(2)}, u32[]{:S(2)}) collective-permute-start(f32[2,4,72,256]{3,2,1,0:T(8,128)} %get-tuple-element.51), channel_id=1, source_target_pairs={{0,4},{8,12},{16,20},{24,28}} | collective-permute-start | bytes 1769480 | tf_op jit(solution)/shard_map/ppermute | solution.py:622
  11.1 31.4 %collective-permute-start.2 = (f32[2,4,72,256]{3,2,1,0:T(8,128)}, f32[2,4,72,256]{3,2,1,0:T(8,128)S(1)}, u32[]{:S(2)}, u32[]{:S(2)}) collective-permute-start(f32[2,4,72,256]{3,2,1,0:T(8,128)} %get-tuple-element.52), channel_id=1, source_target_pairs={{0,6},{8,14},{16,22},{24,30}} | collective-permute-start | bytes 1769480 | tf_op jit(solution)/shard_map/ppermute | solution.py:622
  16.1 20.6 %collective-permute-start.3 = (f32[8,32,256]{2,1,0:T(8,128)}, f32[8,32,256]{2,1,0:T(8,128)S(1)}, u32[]{:S(2)}, u32[]{:S(2)}) collective-permute-start(f32[8,32,256]{2,1,0:T(8,128)} %get-tuple-element.54), channel_id=1, source_target_pairs={{4,0},{12,8},{13,9},{20,16},{21,17},{22,18},{28,24},{29,25},{30,26... | collective-permute-start | bytes 786440 | tf_op jit(solution)/shard_map/ppermute | solution.py:633
  17.4 25.4 %collective-permute-start.10 = (f32[8,32,256]{2,1,0:T(8,128)}, f32[8,32,256]{2,1,0:T(8,128)S(1)}, u32[]{:S(2)}, u32[]{:S(2)}) collective-permute-start(f32[8,32,256]{2,1,0:T(8,128)} %get-tuple-element.65), channel_id=1, source_target_pairs={{5,0},{12,9},{13,8},{20,17},{21,16},{23,18},{28,25},{29,24},{30,27... | collective-permute-start | bytes 786440 | tf_op jit(solution)/shard_map/ppermute | solution.py:633
  38.0 17.1 %collective-permute-start.12 = (f32[8,32,256]{2,1,0:T(8,128)}, f32[8,32,256]{2,1,0:T(8,128)}, u32[]{:S(2)}, u32[]{:S(2)}) collective-permute-start(f32[8,32,256]{2,1,0:T(8,128)} %get-tuple-element.67), channel_id=1, source_target_pairs={{7,0},{14,9},{15,8},{21,18},{22,17},{23,16},{28,27},{29,26},{30,25... | collective-permute-start | bytes 786440 | tf_op jit(solution)/shard_map/ppermute | solution.py:633
  55.1 84.0 %all-to-all-start = ((f32[8,7,32,256]{3,2,1,0:T(8,128)}), f32[8,7,32,256]{3,2,1,0:T(8,128)S(1)}, u32[]{:S(2)}, u32[]{:S(2)}) async-start(f32[8,7,32,256]{3,2,1,0:T(8,128)} %pack.4), calls=%async_computation | async-start | bytes 3670016 | tf_op jit(solution)/shard_map/all_to_all | solution.py:599
  64.9 20.1 %collective-permute-start.4 = (f32[4,72,256]{2,1,0:T(8,128)}, f32[4,72,256]{2,1,0:T(8,128)S(1)}, u32[]{:S(2)}, u32[]{:S(2)}) collective-permute-start(f32[4,72,256]{2,1,0:T(8,128)} %slice_bitcast_fusion.1), channel_id=1, source_target_pairs={{0,1},{2,3},{4,5},{6,7},{8,9},{10,11},{12,13},{14,15},{16,17},{18,... | collective-permute-start | bytes 884744 | tf_op jit(solution)/shard_map/ppermute | solution.py:643
  96.5 42.6 %collective-permute-start.9 = (f32[16,32,256]{2,1,0:T(8,128)}, f32[16,32,256]{2,1,0:T(8,128)S(1)}, u32[]{:S(2)}, u32[]{:S(2)}) collective-permute-start(f32[16,32,256]{2,1,0:T(8,128)} %lead_rows.1.refs_0_), channel_id=1, source_target_pairs={{0,2},{1,3},{2,0},{3,1},{4,6},{5,7},{6,4},{7,5},{8,10},{9,11},{10,... | collective-permute-start | bytes 1572872 | tf_op jit(solution)/shard_map/ppermute | solution.py:653
  98.3 40.8 %collective-permute-start.8 = (f32[16,32,256]{2,1,0:T(8,128)}, f32[16,32,256]{2,1,0:T(8,128)}, u32[]{:S(2)}, u32[]{:S(2)}) collective-permute-start(f32[16,32,256]{2,1,0:T(8,128)} %lead_rows.1.refs_0_), channel_id=1, source_target_pairs={{0,4},{1,5},{2,6},{3,7},{4,0},{5,1},{6,2},{7,3},{8,12},{9,13},{10,... | collective-permute-start | bytes 1572872 | tf_op jit(solution)/shard_map/ppermute | solution.py:652
  104.2 29.0 %collective-permute-start.14 = (f32[8,32,256]{2,1,0:T(8,128)}, f32[8,32,256]{2,1,0:T(8,128)S(1)}, u32[]{:S(2)}, u32[]{:S(2)}) collective-permute-start(f32[8,32,256]{2,1,0:T(8,128)} %get-tuple-element.72), channel_id=1, source_target_pairs={{2,0},{10,8},{11,9},{16,18},{18,16},{19,17},{24,26},{25,27},{26,24... | collective-permute-start | bytes 786440 | tf_op jit(solution)/shard_map/ppermute | solution.py:633
  105.5 33.6 %collective-permute-start.15 = (f32[8,32,256]{2,1,0:T(8,128)}, f32[8,32,256]{2,1,0:T(8,128)S(1)}, u32[]{:S(2)}, u32[]{:S(2)}) collective-permute-start(f32[8,32,256]{2,1,0:T(8,128)} %get-tuple-element.74), channel_id=1, source_target_pairs={{3,0},{10,9},{11,8},{17,18},{18,17},{19,16},{24,27},{25,26},{26,25... | collective-permute-start | bytes 786440 | tf_op jit(solution)/shard_map/ppermute | solution.py:633
  140.6 123.4 %all-to-all-start.1 = ((f32[8,21,32,256]{3,2,1,0:T(8,128)}), f32[8,21,32,256]{3,2,1,0:T(8,128)}, u32[]{:S(2)}, u32[]{:S(2)}) async-start(f32[8,21,32,256]{3,2,1,0:T(8,128)} %pack.5), calls=%async_computation.1 | async-start | bytes 11010048 | tf_op jit(solution)/shard_map/all_to_all | solution.py:599
  158.2 102.3 %collective-permute-start.16 = (f32[3,16,32,256]{3,2,1,0:T(8,128)}, f32[3,16,32,256]{3,2,1,0:T(8,128)}, u32[]{:S(2)}, u32[]{:S(2)}) collective-permute-start(f32[3,16,32,256]{3,2,1,0:T(8,128)} %pad_maximum_fusion.1), channel_id=1, source_target_pairs={{0,1},{1,0},{2,3},{3,2},{4,5},{5,4},{6,7},{7,6},{8,9},{9,8},{10,11... | collective-permute-start | bytes 4718600 | tf_op jit(solution)/shard_map/ppermute | solution.py:660
  158.2 86.9 %collective-permute-start.17 = (f32[16,32,256]{2,1,0:T(8,128)}, f32[16,32,256]{2,1,0:T(8,128)S(1)}, u32[]{:S(2)}, u32[]{:S(2)}) collective-permute-start(f32[16,32,256]{2,1,0:T(8,128)} %collective-permute-done.8.refs_2_), channel_id=1, source_target_pairs={{0,2},{1,3},{2,0},{3,1},{4,6},{5,7},{6,4},{7,5},{8,10},{9,11},{10,... | collective-permute-start | bytes 1572872 | tf_op jit(solution)/shard_map/ppermute | solution.py:656
  159.2 94.5 %collective-permute-start.19 = (f32[2,256,256]{2,1,0:T(8,128)}, f32[2,256,256]{2,1,0:T(8,128)}, u32[]{:S(2)}, u32[]{:S(2)}) collective-permute-start(f32[2,256,256]{2,1,0:T(8,128)} %get-tuple-element.82), channel_id=1, source_target_pairs={{0,8},{8,16},{16,24},{24,0},{1,9},{9,17},{17,25},{25,1},{2,10},{10... | collective-permute-start | bytes 1572872 | tf_op jit(solution)/shard_map/ppermute | solution.py:672
  159.2 95.6 %collective-permute-start.20 = (f32[2,256,256]{2,1,0:T(8,128)}, f32[2,256,256]{2,1,0:T(8,128)}, u32[]{:S(2)}, u32[]{:S(2)}) collective-permute-start(f32[2,256,256]{2,1,0:T(8,128)} %get-tuple-element.83), channel_id=1, source_target_pairs={{0,16},{8,24},{16,0},{24,8},{1,17},{9,25},{17,1},{25,9},{2,18},{10... | collective-permute-start | bytes 1572872 | tf_op jit(solution)/shard_map/ppermute | solution.py:672
  159.2 96.7 %collective-permute-start.21 = (f32[2,256,256]{2,1,0:T(8,128)}, f32[2,256,256]{2,1,0:T(8,128)S(1)}, u32[]{:S(2)}, u32[]{:S(2)}) collective-permute-start(f32[2,256,256]{2,1,0:T(8,128)} %get-tuple-element.84), channel_id=1, source_target_pairs={{0,24},{8,0},{16,8},{24,16},{1,25},{9,1},{17,9},{25,17},{2,26},{10... | collective-permute-start | bytes 1572872 | tf_op jit(solution)/shard_map/ppermute | solution.py:672
  245.1 15.4 %collective-permute-start.18 = (f32[1,16,32,256]{3,2,1,0:T(8,128)S(1)}, f32[1,16,32,256]{3,2,1,0:T(8,128)}, u32[]{:S(2)}, u32[]{:S(2)}) collective-permute-start(f32[1,16,32,256]{3,2,1,0:T(8,128)S(1)} %bitcast.67), channel_id=1, source_target_pairs={{0,1},{1,0},{2,3},{3,2},{4,5},{5,4},{6,7},{7,6},{8,9},{9,8},{10,11... | collective-permute-start | bytes 1572872 | tf_op jit(solution)/shard_map/ppermute | solution.py:661
  264.0 181.3 %all-to-all-start.2 = ((f32[8,31,32,256]{3,2,1,0:T(8,128)}), f32[8,31,32,256]{3,2,1,0:T(8,128)}, u32[]{:S(2)}, u32[]{:S(2)}) async-start(f32[8,31,32,256]{3,2,1,0:T(8,128)} %pack.7), calls=%async_computation.2 | async-start | bytes 16252928 | tf_op jit(solution)/shard_map/all_to_all | solution.py:599
  285.3 62.9 %collective-permute-start.26 = (f32[8,8,32,256]{3,2,1,0:T(8,128)S(1)}, f32[8,8,32,256]{3,2,1,0:T(8,128)}, u32[]{:S(2)}, u32[]{:S(2)}) collective-permute-start(f32[8,8,32,256]{3,2,1,0:T(8,128)S(1)} %dynamic-slice_bitcast_fusion), channel_id=1, source_target_pairs={{0,16},{9,25},{18,2},{27,11},{4,20},{13,29},{22,6},{31,15}} | collective-permute-start | bytes 6291464 | tf_op jit(solution)/shard_map/ppermute | solution.py:697
  287.4 60.8 %collective-permute-start.25 = (f32[8,8,32,256]{3,2,1,0:T(8,128)S(1)}, f32[8,8,32,256]{3,2,1,0:T(8,128)}, u32[]{:S(2)}, u32[]{:S(2)}) collective-permute-start(f32[8,8,32,256]{3,2,1,0:T(8,128)S(1)} %dynamic-slice_bitcast_fusion), channel_id=1, source_target_pairs={{0,8},{9,17},{18,26},{27,3},{4,12},{13,21},{22,30},{31,7}} | collective-permute-start | bytes 6291464 | tf_op jit(solution)/shard_map/ppermute | solution.py:697
  288.7 59.5 %collective-permute-start.27 = (f32[8,8,32,256]{3,2,1,0:T(8,128)S(1)}, f32[8,8,32,256]{3,2,1,0:T(8,128)}, u32[]{:S(2)}, u32[]{:S(2)}) collective-permute-start(f32[8,8,32,256]{3,2,1,0:T(8,128)S(1)} %dynamic-slice_bitcast_fusion), channel_id=1, source_target_pairs={{0,24},{9,1},{18,10},{27,19},{4,28},{13,5},{22,14},{31,23}} | collective-permute-start | bytes 6291464 | tf_op jit(solution)/shard_map/ppermute | solution.py:697
  445.3 35.3 %all-to-all-start.3 = ((f32[8,5,32,256]{3,2,1,0:T(8,128)}), f32[8,5,32,256]{3,2,1,0:T(8,128)S(1)}, u32[]{:S(2)}, u32[]{:S(2)}) async-start(f32[8,5,32,256]{3,2,1,0:T(8,128)} %pack.6), calls=%async_computation.3 | async-start | bytes 2621440 | tf_op jit(solution)/shard_map/all_to_all | solution.py:599
  (29 other events, 402.5 us)
where the time goes:
time: 498 us; the launch traced here: 489 us
  waiting for transfers between devices  227 us (46%)
  Pallas kernels  113 us (23%)
  other arithmetic  69.2 us (14%)
  starting transfers between devices  60.1 us (12%)
  local copies, waits for them, and re-layouts  11 us (2%)
  blocking collectives  5.48 us (1%)
    ppermute x1, waiting for transfers between devices, on_device(): outer = [lax.ppermute(across, 'col', across_col(k)) for k in steps]  84.1 us
    all_to_all x4, waiting for transfers between devices, exchange(): lax.all_to_all(blocks, 'col', split_axis=0, concat_axis=0, tiled=True)  67.9 us
    ppermute x7, waiting for transfers between devices, send_edge(): return lax.ppermute(value, ('row', 'col'), steps)  58.1 us
    pallas_call x4, Pallas kernels, finish(): pl.pallas_call(functools.partial(finish_kernel, depths, shared, edges, ro...  51.4 us
    another operation x4, other arithmetic, both(): return (factor, jax.scipy.linalg.solve_triangular(factor, eye, lower=True))  29.6 us
    another operation x6, other arithmetic, both(): factor = lax.linalg.cholesky(block, symmetrize_input=False)  24.8 us
    pallas_call x4, Pallas kernels, pack(): pl.pallas_call(functools.partial(pack_kernel, depths, counts), out_shape=...  23.5 us
    all_to_all x4, starting transfers between devices, exchange(): lax.all_to_all(blocks, 'col', split_axis=0, concat_axis=0, tiled=True)  22.2 us
  transfers between devices with their start and end apart: 32, of which 14 were waited for; matrix products, arithmetic and copies ran while one was open for 16% of the time, Pallas kernels for 20%

commit v1 on v0

--- a/solution.py
+++ b/solution.py
@@ -499,7 +499,8 @@
             store(0, row_buf[slot])
 
         zero = jnp.zeros((width, LANES), jnp.float32)
-        for n in range(nb * halves, stride):
+        filled = counts[i - 2] * halves if i >= 2 else stride
+        for n in range(nb * halves, filled):
             out_buf[slot, pl.ds(n, width, stride=stride), :] = zero
         send(i).start()
     for i in range(max(steps - 2, 0), steps):
@@ -584,10 +585,10 @@
         (a, shared[a]) for a in range(row_tiles) if depth_blocks(a, row_size, col_size) > shared[a]
     ]
     edge_of = {a: i for i, (a, _) in enumerate(edge_blocks)}
-    last = (row_tiles - 5) * 3 // 4 + 1
-    parts = [[row_tiles - 2], [row_tiles - 1, row_tiles - 3, row_tiles - 4]]
-    parts.append([a for a in range(row_tiles - 5, -1, -1) if a != last])
-    parts.append([last])
+    rest = [a for a in range(row_tiles - 1, -1, -1) if a != row_tiles - 2]
+    total = sum(shared[a] for a in rest)
+    deep = next(n for n in range(len(rest)) if 9 * sum(shared[a] for a in rest[:n]) >= 4 * total)
+    parts = [[row_tiles - 2], rest[deep:], rest[:deep]]
 
     def packed(part, *after):
         held = lax.optimization_barrier((front,) + after)[0]
@@ -699,8 +700,6 @@
 
     out = None
     for step, part in enumerate(parts):
-        if step == 2:
-            arrived.append(exchange(packed(parts[3]), arrived[2], out))
         out = finish(
             part,
             [shared[a] for a in part],

time: 498 us -> 502 us (level)
  the two profiles are of different devices: /device:TPU:6 before, /device:TPU:2 now
where the time goes in v1:
time: 502 us; the launch traced here: 494 us
  waiting for transfers between devices  237 us (47%)
  Pallas kernels  110 us (22%)
  starting transfers between devices  67.4 us (13%)
  other arithmetic  60.6 us (12%)
  local copies, waits for them, and re-layouts  9.91 us (2%)
  blocking collectives  5.48 us (1%)
    ppermute x1, waiting for transfers between devices, on_device(): outer = [lax.ppermute(across, 'col', across_col(k)) for k in steps]  121 us
    pallas_call x3, Pallas kernels, finish(): pl.pallas_call(functools.partial(finish_kernel, depths, shared, edges, ro...  51.4 us
    all_to_all x3, waiting for transfers between devices, exchange(): lax.all_to_all(blocks, 'col', split_axis=0, concat_axis=0, tiled=True)  46.8 us
    ppermute x7, waiting for transfers between devices, send_edge(): return lax.ppermute(value, ('row', 'col'), steps)  45.6 us
    another operation x6, other arithmetic, both(): factor = lax.linalg.cholesky(block, symmetrize_input=False)  24.8 us
    pallas_call x3, Pallas kernels, pack(): pl.pallas_call(functools.partial(pack_kernel, depths, counts), out_shape=...  21.2 us
    another operation x4, other arithmetic, both(): return (factor, jax.scipy.linalg.solve_triangular(factor, eye, lower=True))  20.9 us
    all_to_all x3, starting transfers between devices, exchange(): lax.all_to_all(blocks, 'col', split_axis=0, concat_axis=0, tiled=True)  17.5 us
  transfers between devices with their start and end apart: 31, of which 13 were waited for; matrix products, arithmetic and copies ran while one was open for 14% of the time, Pallas kernels for 17%

profile of v1, /device:TPU:2, one launch (start us, length us, event | category | flops | bytes accessed | tf_op | source)
XLA Modules:
  0.0 493.7 jit_solution(17401071427106535290)
XLA Ops:
  1.2 8.4 %move_tiles.1 = (f32[2,256,256]{2,1,0:T(8,128)}, f32[2,256,256]{2,1,0:T(8,128)}, f32[2,256,256]{2,1,0:T(8,128)}, f32[2,256,256]{2,1,0:T(8,128)}, f32[2,4,72,256]...) custom-call(s32[2]{0:T(128)} %pad_add_fusion.ids_ref, ...), custom_call_target="tpu_custom_call" | custom-call | tf_op jit(solution)/shard_map/move_tiles/pallas_call | solution.py:85
  23.6 13.7 %collective-permute-done.3.rest_4_ = f32[8,32,256]{2,1,0:T(8,128)S(1)} collective-permute-done((f32[8,32,256]{2,1,0:T(8,128)}, f32[8,32,256]{2,1,0:T(8,128)S(1)}, u32[]{:S(2)}, u32[]{:S(2)}) %collective-permute-start.3) | collective-permute-done | bytes 262176 | tf_op jit(solution)/shard_map/ppermute | solution.py:634
  43.1 8.2 %collective-permute-done.2 = f32[2,4,72,256]{3,2,1,0:T(8,128)S(1)} collective-permute-done((f32[2,4,72,256]{3,2,1,0:T(8,128)}, f32[2,4,72,256]{3,2,1,0:T(8,128)S(1)}, u32[]{:S(2)}, u32[]{:S(2)}) %collective-permute-start.2) | collective-permute-done | bytes 589856 | tf_op jit(solution)/shard_map/ppermute | solution.py:623
  54.6 7.5 %all-to-all-start = ((f32[8,7,32,256]{3,2,1,0:T(8,128)}), f32[8,7,32,256]{3,2,1,0:T(8,128)S(1)}, u32[]{:S(2)}, u32[]{:S(2)}) async-start(f32[8,7,32,256]{3,2,1,0:T(8,128)} %pack.3), calls=%async_computation | async-start | bytes 3670016 | tf_op jit(solution)/shard_map/all_to_all | solution.py:600
  71.6 9.6 %pack.4 = f32[8,30,32,256]{3,2,1,0:T(8,128)} custom-call(f32[16,1,32,8,8,256]{5,4,3,2,1,0:T(8,128)} %front_ref.5), custom_call_target="tpu_custom_call" | custom-call | tf_op jit(solution)/shard_map/pack/pallas_call | solution.py:326
  110.5 24.3 %collective-permute-done.14.rest_2_ = f32[8,32,256]{2,1,0:T(8,128)S(1)} collective-permute-done((f32[8,32,256]{2,1,0:T(8,128)}, f32[8,32,256]{2,1,0:T(8,128)S(1)}, u32[]{:S(2)}, u32[]{:S(2)}) %collective-permute-start.14) | collective-permute-done | bytes 262176 | tf_op jit(solution)/shard_map/ppermute | solution.py:634
  139.1 5.1 %all-to-all-start.1 = ((f32[8,30,32,256]{3,2,1,0:T(8,128)}), f32[8,30,32,256]{3,2,1,0:T(8,128)}, u32[]{:S(2)}, u32[]{:S(2)}) async-start(f32[8,30,32,256]{3,2,1,0:T(8,128)} %pack.4), calls=%async_computation.1 | async-start | bytes 15728640 | tf_op jit(solution)/shard_map/all_to_all | solution.py:600
  144.2 8.5 %pack.5 = f32[8,27,32,256]{3,2,1,0:T(8,128)} custom-call(f32[16,1,32,8,8,256]{5,4,3,2,1,0:T(8,128)} %front_ref.5), custom_call_target="tpu_custom_call" | custom-call | tf_op jit(solution)/shard_map/pack/pallas_call | solution.py:326
  160.4 120.9 %collective-permute-done.17.refs_3_ = f32[16,32,256]{2,1,0:T(8,128)S(1)} collective-permute-done((f32[16,32,256]{2,1,0:T(8,128)}, f32[16,32,256]{2,1,0:T(8,128)S(1)}, u32[]{:S(2)}, u32[]{:S(2)}) %collective-permute-start.17) | collective-permute-done | bytes 524320 | tf_op jit(solution)/shard_map/ppermute | solution.py:657
  284.8 5.5 %all-gather = s32[4,1,17]{2,1,0:T(1,128)} all-gather(s32[1,1,17]{2,1,0:T(1,128)S(1)} %bitcast.75), channel_id=1, replica_groups=mesh['row'=4,'col'=8] {'row'}, dimensions={0}, use_global_device_ids=true | all-gather | bytes 340 | tf_op jit(solution)/shard_map/all_gather | solution.py:668
  295.6 8.1 %collective-permute-done.18 = f32[1,16,32,256]{3,2,1,0:T(8,128)} collective-permute-done((f32[1,16,32,256]{3,2,1,0:T(8,128)S(1)}, f32[1,16,32,256]{3,2,1,0:T(8,128)}, u32[]{:S(2)}, u32[]{:S(2)}) %collective-permute-start.18) | collective-permute-done | bytes 524320 | tf_op jit(solution)/shard_map/ppermute | solution.py:662
  303.6 11.0 %all-to-all-done.1.recv_ref = f32[8,30,32,256]{3,2,1,0:T(8,128)} async-done(((f32[8,30,32,256]{3,2,1,0:T(8,128)}), f32[8,30,32,256]{3,2,1,0:T(8,128)}, u32[]{:S(2)}, u32[]{:S(2)}) %all-to-all-start.1) | async-done | bytes 7864352 | tf_op jit(solution)/shard_map/all_to_all | solution.py:600
  314.6 4.8 all-to-all-start.2
  322.6 4.5 order_rows.1.rows_ref
  338.7 11.7 %custom-call.8 = f32[128,128]{1,0:T(8,128)S(1)} custom-call(f32[128,128]{1,0:T(8,128)S(1)} %slice.53), custom_call_target="Cholesky" | custom-call | tf_op jit(solution)/shard_map/cholesky/custom-call.1 | solution.py:556
  351.7 9.8 %custom-call.9 = f32[1,128,128]{1,2,0:T(8,128)S(1)} custom-call(f32[1,128,128]{2,1,0:T(8,128)S(1)} %get-tuple-element.91), custom_call_target="InvertDiagBlocksLowerTriangular" | custom-call | tf_op jit(solution)/shard_map/jit(_solve_triangular)/triangular_solve | solution.py:557
  362.4 11.7 %custom-call.10 = f32[128,128]{1,0:T(8,128)S(1)} custom-call(f32[128,128]{1,0:T(8,128)S(1)} %slice_subtract_fusion), custom_call_target="Cholesky" | custom-call | tf_op jit(solution)/shard_map/cholesky/custom-call.1 | solution.py:556
  375.4 9.9 %custom-call.11 = f32[1,128,128]{1,2,0:T(8,128)S(1)} custom-call(f32[1,128,128]{2,1,0:T(8,128)S(1)} %get-tuple-element.89), custom_call_target="InvertDiagBlocksLowerTriangular" | custom-call | tf_op jit(solution)/shard_map/jit(_solve_triangular)/triangular_solve | solution.py:557
  387.2 6.0 %add_add_fusion.cols_ref = f32[8,8,32,256]{3,2,1,0:T(8,128)} fusion(f32[8,8,32,256]{3,2,1,0:T(8,128)} %collective-permute-done.27, f32[8,8,32,256]{3,2,1,0:T(8,128)} %collective-permute-done.26, f32[8,8,32,256]{3,2,1,0:T(8,128)} %collective-permute-done.25, pred[]{:T(512)S(6)} %eq.24, f32[8,8,2,32,256]{4,3,2,1,0:T(8,128)} %bitcast.62, s32[]{:T(128)S(6)} %select_n.69), kind=kLoop, calls=%fused_computation.1 | loop fusion | flops 2097152 | bytes 10485765 | tf_op jit(solution)/shard_map/add | solution.py:698
  393.1 12.9 %panels.1 = (f32[16,256,256]{2,1,0:T(8,128)}, bf16[8,256,256]{2,1,0:T(8,128)(2,1)}, bf16[8,256,256]{2,1,0:T(8,128)(2,1)}) custom-call(s32[2]{0:T(128)} %pad_add_fusion.ids_ref, f32[256,256]{1,0:T(8,128)} %get-tuple-element.98.inverse_ref, f32[256,256]{1,0:T(8,128)} %get-tuple-element.97.factor_ref, f32[8,16,32,256]{3,2,1,0:T(8,128)} %order_rows.1.rows_ref, ...), custom_call_target="tpu_custom_call" | custom-call | tf_op jit(solution)/shard_map/panels/pallas_call | solution.py:263
  406.0 7.3 %finish.3.rest_8_ = f32[16,4096,128]{2,1,0:T(8,128)} custom-call(s32[2]{0:T(128)} %pad_add_fusion.ids_ref, s32[2,8]{1,0:T(2,128)} %locate.1.own_ref, f32[8,7,32,256]{3,2,1,0:T(8,128)} %copy-done.1, f32[16,256,256]{2,1,0:T(8,128)} %get-tuple-element.85.rows_ref, bf16[8,256,256]{2,1,0:T(8,128)(2,1)} %get-tuple-element.86.high_ref, ...), custom_call_target="tpu_custom_call" | custom-call | tf_op jit(solution)/shard_map/finish/pallas_call | solution.py:526
  413.3 24.3 %finish.4.rest_8_ = f32[16,4096,128]{2,1,0:T(8,128)} custom-call(s32[2]{0:T(128)} %pad_add_fusion.ids_ref, s32[2,8]{1,0:T(2,128)} %locate.1.own_ref, f32[8,30,32,256]{3,2,1,0:T(8,128)} %all-to-all-done.1.recv_ref, f32[16,256,256]{2,1,0:T(8,128)} %get-tuple-element.85.rows_ref, ...), custom_call_target="tpu_custom_call", output_to_operand_aliasing={{}: (15, {})} | custom-call | tf_op jit(solution)/shard_map/finish/pallas_call | solution.py:526
  437.6 35.8 %all-to-all-done.2.recv_ref = f32[8,27,32,256]{3,2,1,0:T(8,128)} async-done(((f32[8,27,32,256]{3,2,1,0:T(8,128)}), f32[8,27,32,256]{3,2,1,0:T(8,128)}, u32[]{:S(2)}, u32[]{:S(2)}) %all-to-all-start.2) | async-done | bytes 7077920 | tf_op jit(solution)/shard_map/all_to_all | solution.py:600
  473.4 19.8 %finish.5 = f32[16,4096,128]{2,1,0:T(8,128)} custom-call(s32[2]{0:T(128)} %pad_add_fusion.ids_ref, s32[2,8]{1,0:T(2,128)} %locate.1.own_ref, f32[8,27,32,256]{3,2,1,0:T(8,128)} %all-to-all-done.2.recv_ref, f32[16,256,256]{2,1,0:T(8,128)} %get-tuple-element.85.rows_ref, ...), custom_call_target="tpu_custom_call", output_to_operand_aliasing={{}: (15, {})} | custom-call | tf_op jit(solution)/shard_map/finish/pallas_call | solution.py:526
  (131 shorter events, 102.6 us)
Async XLA Ops:
  9.7 28.9 %collective-permute-start = (f32[2,4,72,256]{3,2,1,0:T(8,128)}, f32[2,4,72,256]{3,2,1,0:T(8,128)S(1)}, u32[]{:S(2)}, u32[]{:S(2)}) collective-permute-start(f32[2,4,72,256]{3,2,1,0:T(8,128)} %get-tuple-element.49), channel_id=1, source_target_pairs={{0,2},{8,10},{16,18},{24,26}} | collective-permute-start | bytes 1769480 | tf_op jit(solution)/shard_map/ppermute | solution.py:623
  13.2 29.9 %collective-permute-start.1 = (f32[2,4,72,256]{3,2,1,0:T(8,128)}, f32[2,4,72,256]{3,2,1,0:T(8,128)S(1)}, u32[]{:S(2)}, u32[]{:S(2)}) collective-permute-start(f32[2,4,72,256]{3,2,1,0:T(8,128)} %get-tuple-element.50), channel_id=1, source_target_pairs={{0,4},{8,12},{16,20},{24,28}} | collective-permute-start | bytes 1769480 | tf_op jit(solution)/shard_map/ppermute | solution.py:623
  14.9 36.4 %collective-permute-start.2 = (f32[2,4,72,256]{3,2,1,0:T(8,128)}, f32[2,4,72,256]{3,2,1,0:T(8,128)S(1)}, u32[]{:S(2)}, u32[]{:S(2)}) collective-permute-start(f32[2,4,72,256]{3,2,1,0:T(8,128)} %get-tuple-element.51), channel_id=1, source_target_pairs={{0,6},{8,14},{16,22},{24,30}} | collective-permute-start | bytes 1769480 | tf_op jit(solution)/shard_map/ppermute | solution.py:623
  21.0 16.3 %collective-permute-start.3 = (f32[8,32,256]{2,1,0:T(8,128)}, f32[8,32,256]{2,1,0:T(8,128)S(1)}, u32[]{:S(2)}, u32[]{:S(2)}) collective-permute-start(f32[8,32,256]{2,1,0:T(8,128)} %get-tuple-element.53), channel_id=1, source_target_pairs={{4,0},{12,8},{13,9},{20,16},{21,17},{22,18},{28,24},{29,25},{30,26... | collective-permute-start | bytes 786440 | tf_op jit(solution)/shard_map/ppermute | solution.py:634
  22.3 32.3 %collective-permute-start.10 = (f32[8,32,256]{2,1,0:T(8,128)}, f32[8,32,256]{2,1,0:T(8,128)S(1)}, u32[]{:S(2)}, u32[]{:S(2)}) collective-permute-start(f32[8,32,256]{2,1,0:T(8,128)} %get-tuple-element.64), channel_id=1, source_target_pairs={{5,0},{12,9},{13,8},{20,17},{21,16},{23,18},{28,25},{29,24},{30,27... | collective-permute-start | bytes 786440 | tf_op jit(solution)/shard_map/ppermute | solution.py:634
  37.3 17.2 %collective-permute-start.11 = (f32[8,32,256]{2,1,0:T(8,128)}, f32[8,32,256]{2,1,0:T(8,128)S(1)}, u32[]{:S(2)}, u32[]{:S(2)}) collective-permute-start(f32[8,32,256]{2,1,0:T(8,128)} %get-tuple-element.65), channel_id=1, source_target_pairs={{6,0},{14,8},{15,9},{20,18},{22,16},{23,17},{28,26},{29,27},{30,24... | collective-permute-start | bytes 786440 | tf_op jit(solution)/shard_map/ppermute | solution.py:634
  38.6 15.9 %collective-permute-start.12 = (f32[8,32,256]{2,1,0:T(8,128)}, f32[8,32,256]{2,1,0:T(8,128)}, u32[]{:S(2)}, u32[]{:S(2)}) collective-permute-start(f32[8,32,256]{2,1,0:T(8,128)} %get-tuple-element.66), channel_id=1, source_target_pairs={{7,0},{14,9},{15,8},{21,18},{22,17},{23,16},{28,27},{29,26},{30,25... | collective-permute-start | bytes 786440 | tf_op jit(solution)/shard_map/ppermute | solution.py:634
  54.6 83.1 %all-to-all-start = ((f32[8,7,32,256]{3,2,1,0:T(8,128)}), f32[8,7,32,256]{3,2,1,0:T(8,128)S(1)}, u32[]{:S(2)}, u32[]{:S(2)}) async-start(f32[8,7,32,256]{3,2,1,0:T(8,128)} %pack.3), calls=%async_computation | async-start | bytes 3670016 | tf_op jit(solution)/shard_map/all_to_all | solution.py:600
  64.6 19.4 %collective-permute-start.4 = (f32[4,72,256]{2,1,0:T(8,128)}, f32[4,72,256]{2,1,0:T(8,128)S(1)}, u32[]{:S(2)}, u32[]{:S(2)}) collective-permute-start(f32[4,72,256]{2,1,0:T(8,128)} %slice_bitcast_fusion.1), channel_id=1, source_target_pairs={{0,1},{2,3},{4,5},{6,7},{8,9},{10,11},{12,13},{14,15},{16,17},{18,... | collective-permute-start | bytes 884744 | tf_op jit(solution)/shard_map/ppermute | solution.py:644
  95.7 42.0 %collective-permute-start.9 = (f32[16,32,256]{2,1,0:T(8,128)}, f32[16,32,256]{2,1,0:T(8,128)S(1)}, u32[]{:S(2)}, u32[]{:S(2)}) collective-permute-start(f32[16,32,256]{2,1,0:T(8,128)} %lead_rows.1.refs_0_), channel_id=1, source_target_pairs={{0,2},{1,3},{2,0},{3,1},{4,6},{5,7},{6,4},{7,5},{8,10},{9,11},{10,... | collective-permute-start | bytes 1572872 | tf_op jit(solution)/shard_map/ppermute | solution.py:654
  97.4 40.3 %collective-permute-start.8 = (f32[16,32,256]{2,1,0:T(8,128)}, f32[16,32,256]{2,1,0:T(8,128)}, u32[]{:S(2)}, u32[]{:S(2)}) collective-permute-start(f32[16,32,256]{2,1,0:T(8,128)} %lead_rows.1.refs_0_), channel_id=1, source_target_pairs={{0,4},{1,5},{2,6},{3,7},{4,0},{5,1},{6,2},{7,3},{8,12},{9,13},{10,... | collective-permute-start | bytes 1572872 | tf_op jit(solution)/shard_map/ppermute | solution.py:653
  105.8 29.0 %collective-permute-start.14 = (f32[8,32,256]{2,1,0:T(8,128)}, f32[8,32,256]{2,1,0:T(8,128)S(1)}, u32[]{:S(2)}, u32[]{:S(2)}) collective-permute-start(f32[8,32,256]{2,1,0:T(8,128)} %get-tuple-element.71), channel_id=1, source_target_pairs={{2,0},{10,8},{11,9},{16,18},{18,16},{19,17},{24,26},{25,27},{26,24... | collective-permute-start | bytes 786440 | tf_op jit(solution)/shard_map/ppermute | solution.py:634
  107.7 29.9 %collective-permute-start.15 = (f32[8,32,256]{2,1,0:T(8,128)}, f32[8,32,256]{2,1,0:T(8,128)S(1)}, u32[]{:S(2)}, u32[]{:S(2)}) collective-permute-start(f32[8,32,256]{2,1,0:T(8,128)} %get-tuple-element.73), channel_id=1, source_target_pairs={{3,0},{10,9},{11,8},{17,18},{18,17},{19,16},{24,27},{25,26},{26,25... | collective-permute-start | bytes 786440 | tf_op jit(solution)/shard_map/ppermute | solution.py:634
  139.1 175.5 %all-to-all-start.1 = ((f32[8,30,32,256]{3,2,1,0:T(8,128)}), f32[8,30,32,256]{3,2,1,0:T(8,128)}, u32[]{:S(2)}, u32[]{:S(2)}) async-start(f32[8,30,32,256]{3,2,1,0:T(8,128)} %pack.4), calls=%async_computation.1 | async-start | bytes 15728640 | tf_op jit(solution)/shard_map/all_to_all | solution.py:600
  155.2 148.4 %collective-permute-start.16 = (f32[3,16,32,256]{3,2,1,0:T(8,128)}, f32[3,16,32,256]{3,2,1,0:T(8,128)}, u32[]{:S(2)}, u32[]{:S(2)}) collective-permute-start(f32[3,16,32,256]{3,2,1,0:T(8,128)} %pad_maximum_fusion.1), channel_id=1, source_target_pairs={{0,1},{1,0},{2,3},{3,2},{4,5},{5,4},{6,7},{7,6},{8,9},{9,8},{10,11... | collective-permute-start | bytes 4718600 | tf_op jit(solution)/shard_map/ppermute | solution.py:661
  158.1 123.1 %collective-permute-start.17 = (f32[16,32,256]{2,1,0:T(8,128)}, f32[16,32,256]{2,1,0:T(8,128)S(1)}, u32[]{:S(2)}, u32[]{:S(2)}) collective-permute-start(f32[16,32,256]{2,1,0:T(8,128)} %collective-permute-done.8.refs_2_), channel_id=1, source_target_pairs={{0,2},{1,3},{2,0},{3,1},{4,6},{5,7},{6,4},{7,5},{8,10},{9,11},{10,... | collective-permute-start | bytes 1572872 | tf_op jit(solution)/shard_map/ppermute | solution.py:657
  158.6 134.7 %collective-permute-start.19 = (f32[2,256,256]{2,1,0:T(8,128)}, f32[2,256,256]{2,1,0:T(8,128)}, u32[]{:S(2)}, u32[]{:S(2)}) collective-permute-start(f32[2,256,256]{2,1,0:T(8,128)} %get-tuple-element.81), channel_id=1, source_target_pairs={{0,8},{8,16},{16,24},{24,0},{1,9},{9,17},{17,25},{25,1},{2,10},{10... | collective-permute-start | bytes 1572872 | tf_op jit(solution)/shard_map/ppermute | solution.py:673
  158.6 135.8 %collective-permute-start.20 = (f32[2,256,256]{2,1,0:T(8,128)}, f32[2,256,256]{2,1,0:T(8,128)}, u32[]{:S(2)}, u32[]{:S(2)}) collective-permute-start(f32[2,256,256]{2,1,0:T(8,128)} %get-tuple-element.82), channel_id=1, source_target_pairs={{0,16},{8,24},{16,0},{24,8},{1,17},{9,25},{17,1},{25,9},{2,18},{10... | collective-permute-start | bytes 1572872 | tf_op jit(solution)/shard_map/ppermute | solution.py:673
  158.6 136.9 %collective-permute-start.21 = (f32[2,256,256]{2,1,0:T(8,128)}, f32[2,256,256]{2,1,0:T(8,128)S(1)}, u32[]{:S(2)}, u32[]{:S(2)}) collective-permute-start(f32[2,256,256]{2,1,0:T(8,128)} %get-tuple-element.83), channel_id=1, source_target_pairs={{0,24},{8,0},{16,8},{24,16},{1,25},{9,1},{17,9},{25,17},{2,26},{10... | collective-permute-start | bytes 1572872 | tf_op jit(solution)/shard_map/ppermute | solution.py:673
  281.3 22.4 %collective-permute-start.18 = (f32[1,16,32,256]{3,2,1,0:T(8,128)S(1)}, f32[1,16,32,256]{3,2,1,0:T(8,128)}, u32[]{:S(2)}, u32[]{:S(2)}) collective-permute-start(f32[1,16,32,256]{3,2,1,0:T(8,128)S(1)} %bitcast.67), channel_id=1, source_target_pairs={{0,1},{1,0},{2,3},{3,2},{4,5},{5,4},{6,7},{7,6},{8,9},{9,8},{10,11... | collective-permute-start | bytes 1572872 | tf_op jit(solution)/shard_map/ppermute | solution.py:662
  314.6 158.8 %all-to-all-start.2 = ((f32[8,27,32,256]{3,2,1,0:T(8,128)}), f32[8,27,32,256]{3,2,1,0:T(8,128)}, u32[]{:S(2)}, u32[]{:S(2)}) async-start(f32[8,27,32,256]{3,2,1,0:T(8,128)} %pack.5), calls=%async_computation.2 | async-start | bytes 14155776 | tf_op jit(solution)/shard_map/all_to_all | solution.py:600
  332.7 54.4 %collective-permute-start.26 = (f32[8,8,32,256]{3,2,1,0:T(8,128)S(1)}, f32[8,8,32,256]{3,2,1,0:T(8,128)}, u32[]{:S(2)}, u32[]{:S(2)}) collective-permute-start(f32[8,8,32,256]{3,2,1,0:T(8,128)S(1)} %dynamic-slice_bitcast_fusion), channel_id=1, source_target_pairs={{0,16},{9,25},{18,2},{27,11},{4,20},{13,29},{22,6},{31,15}} | collective-permute-start | bytes 6291464 | tf_op jit(solution)/shard_map/ppermute | solution.py:698
  334.0 53.1 %collective-permute-start.25 = (f32[8,8,32,256]{3,2,1,0:T(8,128)S(1)}, f32[8,8,32,256]{3,2,1,0:T(8,128)}, u32[]{:S(2)}, u32[]{:S(2)}) collective-permute-start(f32[8,8,32,256]{3,2,1,0:T(8,128)S(1)} %dynamic-slice_bitcast_fusion), channel_id=1, source_target_pairs={{0,8},{9,17},{18,26},{27,3},{4,12},{13,21},{22,30},{31,7}} | collective-permute-start | bytes 6291464 | tf_op jit(solution)/shard_map/ppermute | solution.py:698
  336.1 51.1 %collective-permute-start.27 = (f32[8,8,32,256]{3,2,1,0:T(8,128)S(1)}, f32[8,8,32,256]{3,2,1,0:T(8,128)}, u32[]{:S(2)}, u32[]{:S(2)}) collective-permute-start(f32[8,8,32,256]{3,2,1,0:T(8,128)S(1)} %dynamic-slice_bitcast_fusion), channel_id=1, source_target_pairs={{0,24},{9,1},{18,10},{27,19},{4,28},{13,5},{22,14},{31,23}} | collective-permute-start | bytes 6291464 | tf_op jit(solution)/shard_map/ppermute | solution.py:698
  (27 other events, 446.5 us)

commit v2 on v0

--- a/solution.py
+++ b/solution.py
@@ -672,7 +672,7 @@
         + [lax.ppermute(moved[shift], "row", along_row(shift)) for shift in range(1, row_size)]
     )
 
-    arrived.append(exchange(third, arrived[1], beside, outside, own, kids))
+    arrived.append(exchange(third, arrived[1], beside, outside, kids))
     edge = [edge[0], *near, *far]
 
     corner_mine = corner = raw_rows[:, 0].reshape(width, width)

time: 498 us -> 498 us (level)
  Pallas kernels: 113 us -> 118 us
    all_to_all x4, waiting for transfers between devices: 67.9 us -> 54 us  [exchange(): lax.all_to_all(blocks, 'col', split_axis=0, concat_axis=0, tiled=True)]
    ppermute x1, waiting for transfers between devices: 4.53 us -> 14.4 us  [on_device(): outside = lax.ppermute(jnp.stack(outer), 'col', across_col(1))]
  transfers between devices with their start and end apart: 32 -> 32, of which waited for: 14 -> 14; matrix products, arithmetic and copies ran while one was open for 16% -> 15% of each run, Pallas kernels for 20% -> 21%
where the time goes in v2:
time: 498 us; the launch traced here: 489 us
  waiting for transfers between devices  224 us (45%)
  Pallas kernels  118 us (24%)
  other arithmetic  67.9 us (14%)
  starting transfers between devices  60.1 us (12%)
  local copies, waits for them, and re-layouts  8.53 us (2%)
  blocking collectives  7.4 us (1%)
    ppermute x1, waiting for transfers between devices, on_device(): outer = [lax.ppermute(across, 'col', across_col(k)) for k in steps]  85 us
    ppermute x7, waiting for transfers between devices, send_edge(): return lax.ppermute(value, ('row', 'col'), steps)  58 us
    pallas_call x4, Pallas kernels, finish(): pl.pallas_call(functools.partial(finish_kernel, depths, shared, edges, ro...  56.3 us
    all_to_all x4, waiting for transfers between devices, exchange(): lax.all_to_all(blocks, 'col', split_axis=0, concat_axis=0, tiled=True)  54 us
    another operation x4, other arithmetic, both(): return (factor, jax.scipy.linalg.solve_triangular(factor, eye, lower=True))  29.6 us
    another operation x6, other arithmetic, both(): factor = lax.linalg.cholesky(block, symmetrize_input=False)  24.8 us
    pallas_call x4, Pallas kernels, pack(): pl.pallas_call(functools.partial(pack_kernel, depths, counts), out_shape=...  23.6 us
    all_to_all x4, starting transfers between devices, exchange(): lax.all_to_all(blocks, 'col', split_axis=0, concat_axis=0, tiled=True)  22.2 us
  transfers between devices with their start and end apart: 32, of which 14 were waited for; matrix products, arithmetic and copies ran while one was open for 15% of the time, Pallas kernels for 21%

profile of v2, /device:TPU:6, one launch (start us, length us, event | category | flops | bytes accessed | tf_op | source)
XLA Modules:
  0.0 488.8 jit_solution(2601418385421743968)
XLA Ops:
  1.2 8.4 %move_tiles.1 = (f32[2,256,256]{2,1,0:T(8,128)}, f32[2,256,256]{2,1,0:T(8,128)}, f32[2,256,256]{2,1,0:T(8,128)}, f32[2,256,256]{2,1,0:T(8,128)}, f32[2,4,72,256]...) custom-call(s32[2]{0:T(128)} %pad_add_fusion.ids_ref, ...), custom_call_target="tpu_custom_call" | custom-call | tf_op jit(solution)/shard_map/move_tiles/pallas_call | solution.py:85
  18.8 18.0 %collective-permute-done.3.rest_4_ = f32[8,32,256]{2,1,0:T(8,128)S(1)} collective-permute-done((f32[8,32,256]{2,1,0:T(8,128)}, f32[8,32,256]{2,1,0:T(8,128)S(1)}, u32[]{:S(2)}, u32[]{:S(2)}) %collective-permute-start.3) | collective-permute-done | bytes 262176 | tf_op jit(solution)/shard_map/ppermute | solution.py:633
  42.9 6.2 %collective-permute-done.11.rest_6_ = f32[8,32,256]{2,1,0:T(8,128)S(1)} collective-permute-done((f32[8,32,256]{2,1,0:T(8,128)}, f32[8,32,256]{2,1,0:T(8,128)S(1)}, u32[]{:S(2)}, u32[]{:S(2)}) %collective-permute-start.11) | collective-permute-done | bytes 262176 | tf_op jit(solution)/shard_map/ppermute | solution.py:633
  49.1 6.1 %collective-permute-done.12.rest_7_ = f32[8,32,256]{2,1,0:T(8,128)} collective-permute-done((f32[8,32,256]{2,1,0:T(8,128)}, f32[8,32,256]{2,1,0:T(8,128)}, u32[]{:S(2)}, u32[]{:S(2)}) %collective-permute-start.12) | collective-permute-done | bytes 262176 | tf_op jit(solution)/shard_map/ppermute | solution.py:633
  55.2 7.5 %all-to-all-start = ((f32[8,7,32,256]{3,2,1,0:T(8,128)}), f32[8,7,32,256]{3,2,1,0:T(8,128)S(1)}, u32[]{:S(2)}, u32[]{:S(2)}) async-start(f32[8,7,32,256]{3,2,1,0:T(8,128)} %pack.4), calls=%async_computation | async-start | bytes 3670016 | tf_op jit(solution)/shard_map/all_to_all | solution.py:599
  69.5 7.5 %pack.5 = f32[8,21,32,256]{3,2,1,0:T(8,128)} custom-call(f32[16,1,32,8,8,256]{5,4,3,2,1,0:T(8,128)} %front_ref.6), custom_call_target="tpu_custom_call" | custom-call | tf_op jit(solution)/shard_map/pack/pallas_call | solution.py:326
  77.0 8.1 %collective-permute-done.4 = f32[4,72,256]{2,1,0:T(8,128)S(1)} collective-permute-done((f32[4,72,256]{2,1,0:T(8,128)}, f32[4,72,256]{2,1,0:T(8,128)S(1)}, u32[]{:S(2)}, u32[]{:S(2)}) %collective-permute-start.4) | collective-permute-done | bytes 294944 | tf_op jit(solution)/shard_map/ppermute | solution.py:643
  105.6 6.0 %collective-permute-start.15 = (f32[8,32,256]{2,1,0:T(8,128)}, f32[8,32,256]{2,1,0:T(8,128)S(1)}, u32[]{:S(2)}, u32[]{:S(2)}) collective-permute-start(f32[8,32,256]{2,1,0:T(8,128)} %get-tuple-element.74), channel_id=1, source_target_pairs={{3,0},{10,9},{11,8},{17,18},{18,17},{19,16},{24,27},{25,26},{26,25... | collective-permute-start | bytes 786440 | tf_op jit(solution)/shard_map/ppermute | solution.py:633
  111.6 21.7 %collective-permute-done.14.rest_2_ = f32[8,32,256]{2,1,0:T(8,128)S(1)} collective-permute-done((f32[8,32,256]{2,1,0:T(8,128)}, f32[8,32,256]{2,1,0:T(8,128)S(1)}, u32[]{:S(2)}, u32[]{:S(2)}) %collective-permute-start.14) | collective-permute-done | bytes 262176 | tf_op jit(solution)/shard_map/ppermute | solution.py:633
  145.6 10.3 %pack.7 = f32[8,31,32,256]{3,2,1,0:T(8,128)} custom-call(f32[16,1,32,8,8,256]{5,4,3,2,1,0:T(8,128)} %front_ref.6), custom_call_target="tpu_custom_call" | custom-call | tf_op jit(solution)/shard_map/pack/pallas_call | solution.py:326
  160.1 85.0 %collective-permute-done.17.refs_3_ = f32[16,32,256]{2,1,0:T(8,128)S(1)} collective-permute-done((f32[16,32,256]{2,1,0:T(8,128)}, f32[16,32,256]{2,1,0:T(8,128)S(1)}, u32[]{:S(2)}, u32[]{:S(2)}) %collective-permute-start.17) | collective-permute-done | bytes 524320 | tf_op jit(solution)/shard_map/ppermute | solution.py:656
  245.9 14.4 %collective-permute-done.18 = f32[1,16,32,256]{3,2,1,0:T(8,128)S(1)} collective-permute-done((f32[1,16,32,256]{3,2,1,0:T(8,128)S(1)}, f32[1,16,32,256]{3,2,1,0:T(8,128)S(1)}, u32[]{:S(2)}, u32[]{:S(2)}) %collective-permute-start.18) | collective-permute-done | bytes 524320 | tf_op jit(solution)/shard_map/ppermute | solution.py:661
  283.4 7.4 %all-gather = s32[4,1,17]{2,1,0:T(1,128)} all-gather(s32[1,1,17]{2,1,0:T(1,128)S(1)} %bitcast.75), channel_id=1, replica_groups=mesh['row'=4,'col'=8] {'row'}, dimensions={0}, use_global_device_ids=true | all-gather | bytes 340 | tf_op jit(solution)/shard_map/all_gather | solution.py:667
  300.1 11.7 %custom-call.8 = f32[128,128]{1,0:T(8,128)S(1)} custom-call(f32[128,128]{1,0:T(8,128)S(1)} %slice.53), custom_call_target="Cholesky" | custom-call | tf_op jit(solution)/shard_map/cholesky/custom-call.1 | solution.py:555
  313.1 9.8 %custom-call.9 = f32[1,128,128]{1,2,0:T(8,128)S(1)} custom-call(f32[1,128,128]{2,1,0:T(8,128)S(1)} %get-tuple-element.93), custom_call_target="InvertDiagBlocksLowerTriangular" | custom-call | tf_op jit(solution)/shard_map/jit(_solve_triangular)/triangular_solve | solution.py:556
  323.9 11.7 %custom-call.10 = f32[128,128]{1,0:T(8,128)S(1)} custom-call(f32[128,128]{1,0:T(8,128)S(1)} %slice_subtract_fusion), custom_call_target="Cholesky" | custom-call | tf_op jit(solution)/shard_map/cholesky/custom-call.1 | solution.py:555
  337.0 18.5 %custom-call.11 = f32[1,128,128]{1,2,0:T(8,128)S(1)} custom-call(f32[1,128,128]{2,1,0:T(8,128)S(1)} %get-tuple-element.91), custom_call_target="InvertDiagBlocksLowerTriangular" | custom-call | tf_op jit(solution)/shard_map/jit(_solve_triangular)/triangular_solve | solution.py:556
  357.3 6.0 %add_add_fusion.cols_ref = f32[8,8,32,256]{3,2,1,0:T(8,128)} fusion(f32[8,8,32,256]{3,2,1,0:T(8,128)} %collective-permute-done.27, f32[8,8,32,256]{3,2,1,0:T(8,128)} %collective-permute-done.26, f32[8,8,32,256]{3,2,1,0:T(8,128)} %collective-permute-done.25, pred[]{:T(512)S(6)} %eq.24, f32[8,8,2,32,256]{4,3,2,1,0:T(8,128)} %bitcast.62, s32[]{:T(128)S(6)} %select_n.69), kind=kLoop, calls=%fused_computation.1 | loop fusion | flops 2097152 | bytes 10485765 | tf_op jit(solution)/shard_map/add | solution.py:697
  363.3 12.9 %panels.1 = (f32[16,256,256]{2,1,0:T(8,128)}, bf16[8,256,256]{2,1,0:T(8,128)(2,1)}, bf16[8,256,256]{2,1,0:T(8,128)(2,1)}) custom-call(s32[2]{0:T(128)} %pad_add_fusion.ids_ref, f32[256,256]{1,0:T(8,128)} %get-tuple-element.100.inverse_ref, f32[256,256]{1,0:T(8,128)} %get-tuple-element.99.factor_ref, f32[8,16,32,256]{3,2,1,0:T(8,128)} %order_rows.1.rows_ref, ...), custom_call_target="tpu_custom_call" | custom-call | tf_op jit(solution)/shard_map/panels/pallas_call | solution.py:263
  376.2 7.1 %finish.4.rest_8_ = f32[16,4096,128]{2,1,0:T(8,128)} custom-call(s32[2]{0:T(128)} %pad_add_fusion.ids_ref, s32[2,8]{1,0:T(2,128)} %locate.1.own_ref, f32[8,7,32,256]{3,2,1,0:T(8,128)} %copy-done.1, f32[16,256,256]{2,1,0:T(8,128)} %get-tuple-element.86.rows_ref, bf16[8,256,256]{2,1,0:T(8,128)(2,1)} %get-tuple-element.87.high_ref, ...), custom_call_target="tpu_custom_call" | custom-call | tf_op jit(solution)/shard_map/finish/pallas_call | solution.py:525
  383.3 15.1 %finish.5.rest_8_ = f32[16,4096,128]{2,1,0:T(8,128)} custom-call(s32[2]{0:T(128)} %pad_add_fusion.ids_ref, s32[2,8]{1,0:T(2,128)} %locate.1.own_ref, f32[8,21,32,256]{3,2,1,0:T(8,128)} %all-to-all-done.1.recv_ref, f32[16,256,256]{2,1,0:T(8,128)} %get-tuple-element.86.rows_ref, ...), custom_call_target="tpu_custom_call", output_to_operand_aliasing={{}: (15, {})} | custom-call | tf_op jit(solution)/shard_map/finish/pallas_call | solution.py:525
  398.4 46.8 %all-to-all-done.2.recv_ref = f32[8,31,32,256]{3,2,1,0:T(8,128)} async-done(((f32[8,31,32,256]{3,2,1,0:T(8,128)}), f32[8,31,32,256]{3,2,1,0:T(8,128)}, u32[]{:S(2)}, u32[]{:S(2)}) %all-to-all-start.2) | async-done | bytes 8126496 | tf_op jit(solution)/shard_map/all_to_all | solution.py:599
  449.7 27.4 %finish.6.rest_8_ = f32[16,4096,128]{2,1,0:T(8,128)} custom-call(s32[2]{0:T(128)} %pad_add_fusion.ids_ref, s32[2,8]{1,0:T(2,128)} %locate.1.own_ref, f32[8,31,32,256]{3,2,1,0:T(8,128)} %all-to-all-done.2.recv_ref, f32[16,256,256]{2,1,0:T(8,128)} %get-tuple-element.86.rows_ref, ...), custom_call_target="tpu_custom_call", output_to_operand_aliasing={{}: (15, {})} | custom-call | tf_op jit(solution)/shard_map/finish/pallas_call | solution.py:525
  481.8 6.6 %finish.7 = f32[16,4096,128]{2,1,0:T(8,128)} custom-call(s32[2]{0:T(128)} %pad_add_fusion.ids_ref, s32[2,8]{1,0:T(2,128)} %locate.1.own_ref, f32[8,5,32,256]{3,2,1,0:T(8,128)} %copy-done.2, f32[16,256,256]{2,1,0:T(8,128)} %get-tuple-element.86.rows_ref, bf16[8,256,256]{2,1,0:T(8,128)(2,1)} %get-tuple-element.87.high_ref, ...), custom_call_target="tpu_custom_call", output_to_operand_aliasing={{}: (15, {})} | custom-call | tf_op jit(solution)/shard_map/finish/pallas_call | solution.py:525
  (145 shorter events, 106.8 us)
Async XLA Ops:
  9.6 28.4 %collective-permute-start = (f32[2,4,72,256]{3,2,1,0:T(8,128)}, f32[2,4,72,256]{3,2,1,0:T(8,128)S(1)}, u32[]{:S(2)}, u32[]{:S(2)}) collective-permute-start(f32[2,4,72,256]{3,2,1,0:T(8,128)} %get-tuple-element.50), channel_id=1, source_target_pairs={{0,2},{8,10},{16,18},{24,26}} | collective-permute-start | bytes 1769480 | tf_op jit(solution)/shard_map/ppermute | solution.py:622
  10.3 32.2 %collective-permute-start.1 = (f32[2,4,72,256]{3,2,1,0:T(8,128)}, f32[2,4,72,256]{3,2,1,0:T(8,128)S(1)}, u32[]{:S(2)}, u32[]{:S(2)}) collective-permute-start(f32[2,4,72,256]{3,2,1,0:T(8,128)} %get-tuple-element.51), channel_id=1, source_target_pairs={{0,4},{8,12},{16,20},{24,28}} | collective-permute-start | bytes 1769480 | tf_op jit(solution)/shard_map/ppermute | solution.py:622
  11.0 31.6 %collective-permute-start.2 = (f32[2,4,72,256]{3,2,1,0:T(8,128)}, f32[2,4,72,256]{3,2,1,0:T(8,128)S(1)}, u32[]{:S(2)}, u32[]{:S(2)}) collective-permute-start(f32[2,4,72,256]{3,2,1,0:T(8,128)} %get-tuple-element.52), channel_id=1, source_target_pairs={{0,6},{8,14},{16,22},{24,30}} | collective-permute-start | bytes 1769480 | tf_op jit(solution)/shard_map/ppermute | solution.py:622
  16.2 20.6 %collective-permute-start.3 = (f32[8,32,256]{2,1,0:T(8,128)}, f32[8,32,256]{2,1,0:T(8,128)S(1)}, u32[]{:S(2)}, u32[]{:S(2)}) collective-permute-start(f32[8,32,256]{2,1,0:T(8,128)} %get-tuple-element.54), channel_id=1, source_target_pairs={{4,0},{12,8},{13,9},{20,16},{21,17},{22,18},{28,24},{29,25},{30,26... | collective-permute-start | bytes 786440 | tf_op jit(solution)/shard_map/ppermute | solution.py:633
  17.5 25.4 %collective-permute-start.10 = (f32[8,32,256]{2,1,0:T(8,128)}, f32[8,32,256]{2,1,0:T(8,128)S(1)}, u32[]{:S(2)}, u32[]{:S(2)}) collective-permute-start(f32[8,32,256]{2,1,0:T(8,128)} %get-tuple-element.65), channel_id=1, source_target_pairs={{5,0},{12,9},{13,8},{20,17},{21,16},{23,18},{28,25},{29,24},{30,27... | collective-permute-start | bytes 786440 | tf_op jit(solution)/shard_map/ppermute | solution.py:633
  55.2 84.0 %all-to-all-start = ((f32[8,7,32,256]{3,2,1,0:T(8,128)}), f32[8,7,32,256]{3,2,1,0:T(8,128)S(1)}, u32[]{:S(2)}, u32[]{:S(2)}) async-start(f32[8,7,32,256]{3,2,1,0:T(8,128)} %pack.4), calls=%async_computation | async-start | bytes 3670016 | tf_op jit(solution)/shard_map/all_to_all | solution.py:599
  65.0 20.1 %collective-permute-start.4 = (f32[4,72,256]{2,1,0:T(8,128)}, f32[4,72,256]{2,1,0:T(8,128)S(1)}, u32[]{:S(2)}, u32[]{:S(2)}) collective-permute-start(f32[4,72,256]{2,1,0:T(8,128)} %slice_bitcast_fusion.1), channel_id=1, source_target_pairs={{0,1},{2,3},{4,5},{6,7},{8,9},{10,11},{12,13},{14,15},{16,17},{18,... | collective-permute-start | bytes 884744 | tf_op jit(solution)/shard_map/ppermute | solution.py:643
  96.5 42.6 %collective-permute-start.9 = (f32[16,32,256]{2,1,0:T(8,128)}, f32[16,32,256]{2,1,0:T(8,128)S(1)}, u32[]{:S(2)}, u32[]{:S(2)}) collective-permute-start(f32[16,32,256]{2,1,0:T(8,128)} %lead_rows.1.refs_0_), channel_id=1, source_target_pairs={{0,2},{1,3},{2,0},{3,1},{4,6},{5,7},{6,4},{7,5},{8,10},{9,11},{10,... | collective-permute-start | bytes 1572872 | tf_op jit(solution)/shard_map/ppermute | solution.py:653
  98.4 40.8 %collective-permute-start.8 = (f32[16,32,256]{2,1,0:T(8,128)}, f32[16,32,256]{2,1,0:T(8,128)}, u32[]{:S(2)}, u32[]{:S(2)}) collective-permute-start(f32[16,32,256]{2,1,0:T(8,128)} %lead_rows.1.refs_0_), channel_id=1, source_target_pairs={{0,4},{1,5},{2,6},{3,7},{4,0},{5,1},{6,2},{7,3},{8,12},{9,13},{10,... | collective-permute-start | bytes 1572872 | tf_op jit(solution)/shard_map/ppermute | solution.py:652
  104.3 29.0 %collective-permute-start.14 = (f32[8,32,256]{2,1,0:T(8,128)}, f32[8,32,256]{2,1,0:T(8,128)S(1)}, u32[]{:S(2)}, u32[]{:S(2)}) collective-permute-start(f32[8,32,256]{2,1,0:T(8,128)} %get-tuple-element.72), channel_id=1, source_target_pairs={{2,0},{10,8},{11,9},{16,18},{18,16},{19,17},{24,26},{25,27},{26,24... | collective-permute-start | bytes 786440 | tf_op jit(solution)/shard_map/ppermute | solution.py:633
  105.6 33.5 %collective-permute-start.15 = (f32[8,32,256]{2,1,0:T(8,128)}, f32[8,32,256]{2,1,0:T(8,128)S(1)}, u32[]{:S(2)}, u32[]{:S(2)}) collective-permute-start(f32[8,32,256]{2,1,0:T(8,128)} %get-tuple-element.74), channel_id=1, source_target_pairs={{3,0},{10,9},{11,8},{17,18},{18,17},{19,16},{24,27},{25,26},{26,25... | collective-permute-start | bytes 786440 | tf_op jit(solution)/shard_map/ppermute | solution.py:633
  140.6 123.4 %all-to-all-start.1 = ((f32[8,21,32,256]{3,2,1,0:T(8,128)}), f32[8,21,32,256]{3,2,1,0:T(8,128)}, u32[]{:S(2)}, u32[]{:S(2)}) async-start(f32[8,21,32,256]{3,2,1,0:T(8,128)} %pack.5), calls=%async_computation.1 | async-start | bytes 11010048 | tf_op jit(solution)/shard_map/all_to_all | solution.py:599
  157.3 103.1 %collective-permute-start.16 = (f32[3,16,32,256]{3,2,1,0:T(8,128)S(1)}, f32[3,16,32,256]{3,2,1,0:T(8,128)}, u32[]{:S(2)}, u32[]{:S(2)}) collective-permute-start(f32[3,16,32,256]{3,2,1,0:T(8,128)S(1)} %pad_maximum_fusion.1), channel_id=1, source_target_pairs={{0,1},{1,0},{2,3},{3,2},{4,5},{5,4},{6,7},{7,6},{8,9},{9,8},{10,11... | collective-permute-start | bytes 4718600 | tf_op jit(solution)/shard_map/ppermute | solution.py:660
  157.3 87.8 %collective-permute-start.17 = (f32[16,32,256]{2,1,0:T(8,128)}, f32[16,32,256]{2,1,0:T(8,128)S(1)}, u32[]{:S(2)}, u32[]{:S(2)}) collective-permute-start(f32[16,32,256]{2,1,0:T(8,128)} %collective-permute-done.8.refs_2_), channel_id=1, source_target_pairs={{0,2},{1,3},{2,0},{3,1},{4,6},{5,7},{6,4},{7,5},{8,10},{9,11},{10,... | collective-permute-start | bytes 1572872 | tf_op jit(solution)/shard_map/ppermute | solution.py:656
  158.3 86.8 %collective-permute-start.19 = (f32[2,256,256]{2,1,0:T(8,128)S(1)}, f32[2,256,256]{2,1,0:T(8,128)S(1)}, u32[]{:S(2)}, u32[]{:S(2)}) collective-permute-start(f32[2,256,256]{2,1,0:T(8,128)S(1)} %copy-done.24), channel_id=1, source_target_pairs={{0,8},{8,16},{16,24},{24,0},{1,9},{9,17},{17,25},{25,1},{2,10},{10... | collective-permute-start | bytes 1572872 | tf_op jit(solution)/shard_map/ppermute | solution.py:672
  158.3 86.9 %collective-permute-start.20 = (f32[2,256,256]{2,1,0:T(8,128)S(1)}, f32[2,256,256]{2,1,0:T(8,128)S(1)}, u32[]{:S(2)}, u32[]{:S(2)}) collective-permute-start(f32[2,256,256]{2,1,0:T(8,128)S(1)} %copy-done.23), channel_id=1, source_target_pairs={{0,16},{8,24},{16,0},{24,8},{1,17},{9,25},{17,1},{25,9},{2,18},{10... | collective-permute-start | bytes 1572872 | tf_op jit(solution)/shard_map/ppermute | solution.py:672
  158.4 86.9 %collective-permute-start.21 = (f32[2,256,256]{2,1,0:T(8,128)S(1)}, f32[2,256,256]{2,1,0:T(8,128)S(1)}, u32[]{:S(2)}, u32[]{:S(2)}) collective-permute-start(f32[2,256,256]{2,1,0:T(8,128)S(1)} %copy-done.22), channel_id=1, source_target_pairs={{0,24},{8,0},{16,8},{24,16},{1,25},{9,1},{17,9},{25,17},{2,26},{10... | collective-permute-start | bytes 1572872 | tf_op jit(solution)/shard_map/ppermute | solution.py:672
  264.0 181.3 %all-to-all-start.2 = ((f32[8,31,32,256]{3,2,1,0:T(8,128)}), f32[8,31,32,256]{3,2,1,0:T(8,128)}, u32[]{:S(2)}, u32[]{:S(2)}) async-start(f32[8,31,32,256]{3,2,1,0:T(8,128)} %pack.7), calls=%async_computation.2 | async-start | bytes 16252928 | tf_op jit(solution)/shard_map/all_to_all | solution.py:599
  280.6 17.2 %collective-permute-start.24 = (f32[256,256]{0,1:T(8,128)S(1)}, f32[256,256]{0,1:T(8,128)S(1)}, u32[]{:S(2)}, u32[]{:S(2)}) collective-permute-start(f32[256,256]{0,1:T(8,128)S(1)} %copy.28), channel_id=1, source_target_pairs={{0,24},{1,25},{2,26},{3,27},{4,28},{5,29},{6,30},{7,31}} | collective-permute-start | bytes 786440 | tf_op jit(solution)/shard_map/ppermute | solution.py:681
  281.3 18.5 %collective-permute-start.23 = (f32[256,256]{0,1:T(8,128)S(1)}, f32[256,256]{0,1:T(8,128)S(1)}, u32[]{:S(2)}, u32[]{:S(2)}) collective-permute-start(f32[256,256]{0,1:T(8,128)S(1)} %copy.28), channel_id=1, source_target_pairs={{0,16},{1,17},{2,18},{3,19},{4,20},{5,21},{6,22},{7,23}} | collective-permute-start | bytes 786440 | tf_op jit(solution)/shard_map/ppermute | solution.py:681
  294.5 62.8 %collective-permute-start.26 = (f32[8,8,32,256]{3,2,1,0:T(8,128)S(1)}, f32[8,8,32,256]{3,2,1,0:T(8,128)}, u32[]{:S(2)}, u32[]{:S(2)}) collective-permute-start(f32[8,8,32,256]{3,2,1,0:T(8,128)S(1)} %dynamic-slice_bitcast_fusion), channel_id=1, source_target_pairs={{0,16},{9,25},{18,2},{27,11},{4,20},{13,29},{22,6},{31,15}} | collective-permute-start | bytes 6291464 | tf_op jit(solution)/shard_map/ppermute | solution.py:697
  296.5 60.7 %collective-permute-start.25 = (f32[8,8,32,256]{3,2,1,0:T(8,128)S(1)}, f32[8,8,32,256]{3,2,1,0:T(8,128)}, u32[]{:S(2)}, u32[]{:S(2)}) collective-permute-start(f32[8,8,32,256]{3,2,1,0:T(8,128)S(1)} %dynamic-slice_bitcast_fusion), channel_id=1, source_target_pairs={{0,8},{9,17},{18,26},{27,3},{4,12},{13,21},{22,30},{31,7}} | collective-permute-start | bytes 6291464 | tf_op jit(solution)/shard_map/ppermute | solution.py:697
  297.8 59.5 %collective-permute-start.27 = (f32[8,8,32,256]{3,2,1,0:T(8,128)S(1)}, f32[8,8,32,256]{3,2,1,0:T(8,128)}, u32[]{:S(2)}, u32[]{:S(2)}) collective-permute-start(f32[8,8,32,256]{3,2,1,0:T(8,128)S(1)} %dynamic-slice_bitcast_fusion), channel_id=1, source_target_pairs={{0,24},{9,1},{18,10},{27,19},{4,28},{13,5},{22,14},{31,23}} | collective-permute-start | bytes 6291464 | tf_op jit(solution)/shard_map/ppermute | solution.py:697
  445.3 35.4 %all-to-all-start.3 = ((f32[8,5,32,256]{3,2,1,0:T(8,128)}), f32[8,5,32,256]{3,2,1,0:T(8,128)S(1)}, u32[]{:S(2)}, u32[]{:S(2)}) async-start(f32[8,5,32,256]{3,2,1,0:T(8,128)} %pack.6), calls=%async_computation.3 | async-start | bytes 2621440 | tf_op jit(solution)/shard_map/all_to_all | solution.py:599
  (33 other events, 353.9 us)
